TPU v7x, 32 devices: a whole 2x2x4 slice. The times are simulated.
32 devices in a mesh: dp: 16 (over z, y, core), tensor: 2 (over x).
Axes of the slice: x: 2, y: 2, z: 4, core: 2. Of those that a mesh axis runs over, the one named last changes fastest.
Arguments:
- tokens: bfloat16 [4096, 6144], P('dp', 'tensor'), may hold values from -6 to 6
- grad_out: bfloat16 [4096, 6144], P('dp', 'tensor'), may hold values from -6 to 6
- input_norm_gain: float32 [6144], replicated, may hold values from 0.1 to 1.9
- q_gain: float32 [128], replicated, may hold values from 0.1 to 1.9
- k_gain: float32 [128], replicated, may hold values from 0.1 to 1.9
- w_qkv: bfloat16 [3, 6144, 3072], P(None, 'dp', 'tensor'), may hold values from -0.078125 to 0.078125
- w_out: bfloat16 [3072, 6144], P('tensor', 'dp'), may hold values from -0.109375 to 0.109375
- pattern: int32 [24, 4, 2], P('tensor'), may hold values from 0 to 3, all different within a row
Outputs:
- tokens_grad: bfloat16 [4096, 6144], P('dp', 'tensor')
All inputs are finite; a program needn't handle non-finite values.
Results may differ from a plain program's by a relative error of at most 0.015.
Values may be sent and summed in bfloat16 or wider, within the bound.
A program may use at most 192 MiB of HBM per device.

v0:
```python
import math

import jax
import jax.numpy as jnp
from jax import lax
from jax.sharding import PartitionSpec as P

HD = 128
SEQ = 256
BLK = 64


def norm_rows(values, gain):
    centre = jnp.mean(values, axis=-1, keepdims=True)
    centered_input = values - centre
    inverse_deviation = lax.rsqrt(
        jnp.mean(centered_input * centered_input, axis=-1, keepdims=True) + 1e-06
    )
    return centered_input * inverse_deviation * gain


def block_mask(pattern, seq_len, block):
    count = seq_len // block
    hits = pattern[:, :, :, None] == jnp.arange(count, dtype=jnp.int32)[None, None, None, :]
    allowed = jnp.any(hits, axis=2).astype(jnp.float32)
    heads = allowed.shape[0]
    spread = jnp.broadcast_to(allowed[:, :, None, :, None], (heads, count, block, count, block))
    return spread.reshape(heads, seq_len, seq_len)


def attention_grads(stacked, upstream, q_gain, k_gain, allowed):

    def attend(query, key, value):
        q_normed = norm_rows(query, q_gain)
        k_normed = norm_rows(key, k_gain)
        scores = jnp.einsum(
            "aqhd,akhd->ahqk", q_normed, k_normed, precision=lax.Precision.HIGHEST
        ) / math.sqrt(query.shape[-1])
        weights = jnp.exp(scores) * allowed[None]
        probs = weights / jnp.sum(weights, axis=-1, keepdims=True)
        return jnp.einsum("ahqk,akhd->aqhd", probs, value, precision=lax.Precision.HIGHEST)

    widened = stacked.astype(jnp.float32)
    _, pull = jax.vjp(attend, widened[0], widened[1], widened[2])
    grads = pull(upstream.astype(jnp.float32))
    return jnp.stack(grads).astype(jnp.bfloat16)


def body(tokens, grad_out, input_norm_gain, q_gain, k_gain, w_qkv, w_out, pattern):
    width = tokens.shape[1]
    row_count = tokens.shape[0]
    rows_full, grads_full = (
        lax.all_gather(tokens, "tensor", axis=1, tiled=True),
        lax.all_gather(grad_out, "tensor", axis=1, tiled=True),
    )
    values = rows_full.astype(jnp.float32)
    centre = jnp.mean(values, axis=-1, keepdims=True)
    centered_input = values - centre
    inverse_deviation = lax.rsqrt(
        jnp.mean(centered_input * centered_input, axis=-1, keepdims=True) + 1e-06
    )
    standardized_input = centered_input * inverse_deviation
    normalized_input = (standardized_input * input_norm_gain).astype(jnp.bfloat16)
    whole = lax.all_gather(w_qkv, "dp", axis=1, tiled=True)
    qkv = jnp.einsum(
        "rd,idh->irh", normalized_input, whole, preferred_element_type=jnp.float32
    ).astype(jnp.bfloat16)
    local_width = whole.shape[2]
    upstream = lax.dot_general(
        grads_full,
        lax.all_gather(w_out, "dp", axis=1, tiled=True),
        (((1,), (1,)), ((), ())),
        preferred_element_type=jnp.float32,
    ).astype(jnp.bfloat16)
    local_heads = local_width // HD
    images = row_count // SEQ
    allowed = block_mask(pattern, SEQ, BLK)
    d_qkv = attention_grads(
        qkv.reshape(3, images, SEQ, local_heads, HD),
        upstream.reshape(images, SEQ, local_heads, HD),
        q_gain,
        k_gain,
        allowed,
    )
    d_qkv = d_qkv.reshape(3, row_count, local_width)
    partial_grad = jnp.einsum("irh,idh->rd", d_qkv, whole, preferred_element_type=jnp.float32)
    offset = lax.axis_index("tensor") * width
    d_normed = lax.psum(partial_grad.astype(jnp.bfloat16), "tensor").astype(jnp.float32)
    normalized_gradient = d_normed * input_norm_gain
    leading_term = jnp.mean(normalized_gradient, axis=-1, keepdims=True)
    trailing_term = jnp.mean(normalized_gradient * standardized_input, axis=-1, keepdims=True)
    complete_gradient = inverse_deviation * (
        normalized_gradient - leading_term - standardized_input * trailing_term
    )
    result = lax.dynamic_slice_in_dim(complete_gradient, offset, width, 1)
    return result.astype(jnp.bfloat16)


def solution(mesh):
    return jax.shard_map(
        body,
        mesh=mesh,
        in_specs=(
            P("dp", "tensor"),
            P("dp", "tensor"),
            P(),
            P(),
            P(),
            P(None, "dp", "tensor"),
            P("tensor", "dp"),
            P("tensor", None, None),
        ),
        out_specs=P("dp", "tensor"),
        check_vma=False,
    )
```

profile of v0, /device:TPU:0, one launch (start us, length us, event | category | flops | bytes accessed | tf_op | source)
XLA Modules:
  0.0 674.1 jit_solution(7555071908021062251)
XLA Ops:
  6.5 0.7 all-gather.5.cloned.1.call-update
  7.3 0.0 all-gather.7.cloned.1.call-start
  7.3 0.7 all-gather.7.cloned.1.call-update
  8.0 0.0 all-gather.9.cloned.1.call-start
  8.1 0.7 all-gather.9.cloned.1.call-update
  8.8 0.5 all-gather.11.cloned.1.call-update
  9.3 0.0 all-reduce.2.cloned.1.call-start
  9.4 0.1 copy.49
  9.5 3.6 broadcast_in_dim.14
  13.2 7.0 %broadcast_in_dim_reshape.3 = f32[12,256,256]{1,2,0:T(8,128)} reshape(f32[12,4,64,4,64]{2,1,4,3,0:T(4,128)} %broadcast_in_dim.14) | data formatting | bytes 6291456 | tf_op jit(solution)/shard_map/jvp()/broadcast_in_dim;reshape | solution.py:39
  20.2 36.4 %all-gather.5.cloned.1.call-done = bf16[256,6144]{1,0:T(8,128)(2,1)} async-done(((bf16[256,3072]{1,0:T(8,128)(2,1)}), bf16[256,6144]{1,0:T(8,128)(2,1)}) %all-gather.5.cloned.1.call-update) | async-done | bytes 3145744 | tf_op jit(solution)/shard_map/all_gather | solution.py:53
  56.6 2.5 convert_reduce_fusion
  59.1 0.3 copy-done.3
  59.4 1.0 fusion.3
  60.4 42.7 %all-gather.7.cloned.1.call-done = bf16[256,6144]{1,0:T(8,128)(2,1)} async-done(((bf16[256,3072]{1,0:T(8,128)(2,1)}), bf16[256,6144]{1,0:T(8,128)(2,1)}) %all-gather.7.cloned.1.call-update) | async-done | bytes 3145744 | tf_op jit(solution)/shard_map/all_gather | solution.py:54
  103.1 100.4 %all-gather.9.cloned.1.call-done = bf16[1536,6144]{1,0:T(8,128)(2,1)} async-done(((bf16[1536,384]{1,0:T(8,128)(2,1)}), bf16[1536,6144]{1,0:T(8,128)(2,1)}) %all-gather.9.cloned.1.call-update) | async-done | bytes 18874384 | tf_op jit(solution)/shard_map/all_gather | solution.py:71
  203.5 10.6 %convolution_convert_fusion.1 = bf16[256,1536]{1,0:T(8,128)(2,1)} fusion(bf16[256,6144]{1,0:T(8,128)(2,1)} %all-gather.7.cloned.1.call-done, bf16[1536,6144]{1,0:T(8,128)(2,1)} %all-gather.9.cloned.1.call-done), kind=kOutput, calls=%fused_computation.25 | convolution fusion | flops 4832231424 | bytes 22806528 | tf_op jit(solution)/shard_map/dot_general | solution.py:69
  214.1 2.4 copy.40
  216.5 265.2 %all-gather.11.cloned.1.call-done = bf16[3,6144,1536]{2,1,0:T(8,128)(2,1)} async-done(((bf16[3,384,1536]{2,1,0:T(8,128)(2,1)}), bf16[3,6144,1536]{2,1,0:T(8,128)(2,1)}) %all-gather.11.cloned.1.call-update) | async-done | bytes 56623120 | tf_op jit(solution)/shard_map/all_gather | solution.py:64
  481.7 24.1 %fusion.12 = bf16[3,256,1536]{2,1,0:T(8,128)(2,1)} fusion(bf16[3,6144,1536]{2,1,0:T(8,128)(2,1)} %all-gather.11.cloned.1.call-done, f32[6144]{0:T(1024)S(1)} %copy-done.9, bf16[256,6144]{1,0:T(8,128)(2,1)S(1)} %copy-done.3, f32[256]{0:T(256)S(1)} %add_rsqrt_fusion, f32[256]{0:T(256)S(1)} %broadcast_multiply_fusion.4), kind=kOutput, calls=%fused_computation.23 | convolution fusion | flops 14504558592 | bytes 62154752 | tf_op jit(solution)/shard_map/rd,idh->irh/dot_general | solution.py:65
  505.8 2.9 fusion.50
  508.7 2.1 slice.15
  510.8 0.5 copy.45
  511.2 1.9 copy.43
  513.1 0.1 reduce_sum.126
  513.3 0.1 reduce_sum.128
  513.4 0.2 multiply_reduce_fusion.3
  513.6 0.2 multiply_reduce_fusion.2
  513.8 0.1 copy-done.10
  513.9 1.4 copy-done
  515.3 5.4 fusion.48
  520.7 2.3 copy.41
  523.0 6.4 fusion.25
  529.5 1.0 multiply_reduce_fusion.1
  530.5 0.9 multiply_multiply_fusion
  531.4 5.0 fusion.22
  536.5 3.5 fusion.23
  540.0 2.3 copy.55
  542.3 1.9 fusion.42
  544.3 1.4 add_convert_fusion
  545.6 2.4 copy.54
  548.1 0.4 fusion.41
  548.5 1.3 add_convert_fusion.1
  549.8 1.4 copy.53
  551.2 24.2 %fusion = bf16[256,6144]{1,0:T(8,128)(2,1)} fusion(bf16[3,6144,1536]{2,1,0:T(8,128)(2,1)} %all-gather.11.cloned.1.call-done, bf16[1,256,1536]{2,1,0:T(8,128)(2,1)} %copy.55, bf16[1,256,1536]{2,1,0:T(8,128)(2,1)} %copy.54, bf16[1,256,1536]{2,1,0:T(8,128)(2,1)S(1)} %copy.53), kind=kOutput, calls=%fused_computation.3 | convolution fusion | flops 14499446784 | bytes 62128128 | tf_op jit(solution)/shard_map/irh,idh->rd/dot_general | solution.py:86
  575.4 85.8 %all-reduce.2.cloned.1.call-done = bf16[256,6144]{1,0:T(8,128)(2,1)} async-done(((bf16[256,6144]{1,0:T(8,128)(2,1)}), bf16[256,6144]{1,0:T(8,128)(2,1)}) %all-reduce.2.cloned.1.call-update) | async-done | bytes 3145744 | tf_op jit(solution)/shard_map/psum | solution.py:88
  661.3 4.1 fusion.16
  665.4 2.2 fusion.8
  (41 shorter events, 0.2 us)
Async XLA Ops:
  6.5 50.0 %all-gather.5.cloned.1.call-start = ((), (), s32[]{:S(2)}) async-start(), calls=%async_computation | async-start | bytes 4718592 | tf_op jit(solution)/shard_map/all_gather | solution.py:53
  7.3 95.8 %all-gather.7.cloned.1.call-start = ((), (), s32[]{:S(2)}) async-start(), calls=%async_computation.1 | async-start | bytes 4718592 | tf_op jit(solution)/shard_map/all_gather | solution.py:54
  8.0 1.4 copy-start.12
  8.0 195.5 %all-gather.9.cloned.1.call-start = ((), (), s32[]{:S(2)}) async-start(), calls=%async_computation.2 | async-start | bytes 20054016 | tf_op jit(solution)/shard_map/all_gather | solution.py:71
  8.8 472.9 %all-gather.11.cloned.1.call-start = ((), (), s32[]{:S(2)}) async-start(), calls=%async_computation.3 | async-start | bytes 60162048 | tf_op jit(solution)/shard_map/all_gather | solution.py:64
  9.3 651.9 %all-reduce.2.cloned.1.call-start = ((), (), s32[]{:S(2)}) async-start(), calls=%async_computation.4 | async-start | bytes 6291456 | tf_op jit(solution)/shard_map/psum | solution.py:88
  56.6 2.8 copy-start.3
  60.4 421.3 %copy-start.9 = (f32[6144]{0:T(1024)S(1)}, f32[6144]{0:T(1024)}, u32[]{:S(2)}) copy-start(f32[6144]{0:T(1024)} %param.10) | copy-start | bytes 73732
  513.3 0.7 copy-start.10
  513.3 0.7 copy-start.11
  513.4 1.9 copy-start
  523.0 6.5 copy-start.1
  523.0 6.5 copy-start.2
  523.0 6.5 copy-start.7
  523.0 6.5 copy-start.8
  542.3 2.0 copy-start.6
  545.6 2.4 copy-start.5
  575.4 85.9 %copy-start.4 = (bf16[256,6144]{1,0:T(8,128)(2,1)S(1)}, bf16[256,6144]{1,0:T(8,128)(2,1)}, u32[]{:S(2)}) copy-start(bf16[256,6144]{1,0:T(8,128)(2,1)} %all-gather.5.cloned.1.call-done) | copy-start | bytes 9437188
Sparse Core Ops, SparseCore 0:
  8.9 47.6 all-gather.4
  58.1 44.9 all-gather.6
  104.6 98.8 all-gather.8
  204.9 276.7 all-gather.10
  575.5 85.6 all-reduce.1
where the time goes:
time: 675 us; the launch traced here: 674 us
  waiting for transfers between devices  533 us (79%)
  matrix products  80.3 us (12%)
  local copies, waits for them, and re-layouts  30.7 us (5%)
  other arithmetic  16.4 us (2%)
  between operations  13.4 us (2%)
    all_gather x1, waiting for transfers between devices, body(): whole = lax.all_gather(w_qkv, 'dp', axis=1, tiled=True)  265 us
    all_gather x1, waiting for transfers between devices, body(): lax.all_gather(w_out, 'dp', axis=1, tiled=True)  100 us
    psum x1, waiting for transfers between devices, body(): lax.psum(partial_grad.astype(jnp.bfloat16), 'tensor').astype(jnp.float32)  85.8 us
    all_gather x1, waiting for transfers between devices, body(): lax.all_gather(grad_out, 'tensor', axis=1, tiled=True)  42.7 us
    all_gather x1, waiting for transfers between devices, body(): lax.all_gather(tokens, 'tensor', axis=1, tiled=True)  36.4 us
    dot_general x1, matrix products, body(): jnp.einsum('irh,idh->rd', d_qkv, whole, preferred_element_type=jnp.float32)  24.2 us
    dot_general x1, matrix products, body(): jnp.einsum('rd,idh->irh', normalized_input, whole, preferred_element_type...  24.1 us
    dot_general x3, matrix products, attend(): jnp.einsum('aqhd,akhd->ahqk', q_normed, k_normed, precision=lax.Precision...  14 us
  transfers between devices with their start and end apart: 5, of which 5 were waited for; matrix products, arithmetic and copies ran while one was open for 4% of the time, Pallas kernels for 0%

commit v1 on v0

v1 whole, which is shorter than its diff:
```python
import functools
import math

import jax
import jax.numpy as jnp
from jax import lax
from jax.experimental import pallas as pl
from jax.experimental.pallas import tpu as pltpu
from jax.sharding import PartitionSpec as P

HD = 128
SEQ = 256
BLK = 64
EPS = 1e-06


def attention_kernel(heads, ksel, pattern_ref, q_gain_ref, k_gain_ref, qkv_ref, up_ref, out_ref):
    width = heads * HD
    scale = 1.0 / math.sqrt(HD)
    q_gain = q_gain_ref[...]
    k_gain = k_gain_ref[...]
    blocks = SEQ // BLK
    column_block = lax.broadcasted_iota(jnp.int32, (BLK, SEQ), 1) // BLK

    def normalize(values):
        centred = values - jnp.mean(values, axis=-1, keepdims=True)
        inverse = lax.rsqrt(jnp.mean(centred * centred, axis=-1, keepdims=True) + EPS)
        return centred * inverse, inverse

    def pull_back(grad, hat, inverse, gain):
        d_hat = grad * gain
        return inverse * (
            d_hat
            - jnp.mean(d_hat, axis=-1, keepdims=True)
            - hat * jnp.mean(d_hat * hat, axis=-1, keepdims=True)
        )

    def dot(a, b, dims, precision=None):
        return lax.dot_general(
            a, b, (dims, ((), ())), precision=precision, preferred_element_type=jnp.float32
        )

    for head in range(heads):
        lo = head * HD
        q_hat, q_inverse = normalize(qkv_ref[:, lo : lo + HD].astype(jnp.float32))
        k_hat, k_inverse = normalize(
            qkv_ref[:, width + lo : width + lo + HD].astype(jnp.float32)
        )
        value = qkv_ref[:, 2 * width + lo : 2 * width + lo + HD]
        upstream = up_ref[:, lo : lo + HD]
        q_normed = q_hat * q_gain
        k_normed = k_hat * k_gain
        scores = dot(q_normed * scale, k_normed, ((1,), (1,)), lax.Precision.HIGHEST)
        rows = []
        for i in range(blocks):
            hit = column_block == pattern_ref[(head * blocks + i) * ksel]
            for s in range(1, ksel):
                hit = hit | (column_block == pattern_ref[(head * blocks + i) * ksel + s])
            rows.append(jnp.where(hit, jnp.exp(scores[i * BLK : (i + 1) * BLK]), 0.0))
        weights = jnp.concatenate(rows, axis=0)
        probs = weights / jnp.sum(weights, axis=-1, keepdims=True)
        d_probs = dot(upstream, value, ((1,), (1,)))
        d_value = dot(probs.astype(jnp.bfloat16), upstream, ((0,), (0,)))
        d_scores = probs * (d_probs - jnp.sum(probs * d_probs, axis=-1, keepdims=True))
        d_scores = (d_scores * scale).astype(jnp.bfloat16)
        d_q = dot(d_scores, k_normed.astype(jnp.bfloat16), ((1,), (0,)))
        d_k = dot(d_scores, q_normed.astype(jnp.bfloat16), ((0,), (0,)))
        out_ref[:, lo : lo + HD] = pull_back(d_q, q_hat, q_inverse, q_gain).astype(jnp.bfloat16)
        out_ref[:, width + lo : width + lo + HD] = pull_back(
            d_k, k_hat, k_inverse, k_gain
        ).astype(jnp.bfloat16)
        out_ref[:, 2 * width + lo : 2 * width + lo + HD] = d_value.astype(jnp.bfloat16)


def attention_grads(qkv, upstream, q_gain, k_gain, pattern):
    rows, width = upstream.shape
    heads = width // HD
    images = rows // SEQ
    return pl.pallas_call(
        functools.partial(attention_kernel, heads, pattern.shape[2]),
        grid=(images,),
        out_shape=jax.ShapeDtypeStruct((rows, 3 * width), jnp.bfloat16),
        in_specs=[
            pl.BlockSpec(memory_space=pltpu.SMEM),
            pl.BlockSpec((1, HD), lambda i: (0, 0)),
            pl.BlockSpec((1, HD), lambda i: (0, 0)),
            pl.BlockSpec((SEQ, 3 * width), lambda i: (i, 0)),
            pl.BlockSpec((SEQ, width), lambda i: (i, 0)),
        ],
        out_specs=pl.BlockSpec((SEQ, 3 * width), lambda i: (i, 0)),
        cost_estimate=pl.CostEstimate(
            flops=images * heads * 20 * SEQ * SEQ * HD,
            bytes_accessed=rows * width * 14,
            transcendentals=images * heads * SEQ * SEQ,
        ),
    )(pattern.reshape(-1), q_gain.reshape(1, HD), k_gain.reshape(1, HD), qkv, upstream)


def head_chunks(heads):
    sizes = []
    left = heads - 1
    while left > 0:
        take = min(4, left)
        sizes.append(take)
        left -= take
    return sizes + [1]


def body(tokens, grad_out, input_norm_gain, q_gain, k_gain, w_qkv, w_out, pattern):
    row_count, width = tokens.shape
    parts = lax.axis_size("tensor")
    me = lax.axis_index("tensor")
    local_heads = w_qkv.shape[2] // HD

    w_out_t = w_out.T
    gathered = []
    start = 0
    sizes = head_chunks(local_heads)
    for size in sizes:
        cols = slice(start * HD, (start + size) * HD)
        piece = jnp.concatenate(
            [w_qkv[0, :, cols], w_qkv[1, :, cols], w_qkv[2, :, cols], w_out_t[:, cols]], axis=1
        )
        gathered.append(lax.all_gather(piece, "dp", axis=0, tiled=True))
        start += size

    def exchange(value, shift):
        return lax.ppermute(
            value, "tensor", [(source, (source + shift) % parts) for source in range(parts)]
        )

    def whole_rows(own):
        full = jnp.zeros((row_count, width * parts), own.dtype)
        full = lax.dynamic_update_slice_in_dim(full, own, me * width, 1)
        for shift in range(1, parts):
            full = lax.dynamic_update_slice_in_dim(
                full, exchange(own, shift), lax.rem(me + parts - shift, parts) * width, 1
            )
        return full

    values = whole_rows(tokens).astype(jnp.float32)
    grads_full = whole_rows(grad_out)
    centre = jnp.mean(values, axis=-1, keepdims=True)
    centred = values - centre
    inverse = lax.rsqrt(jnp.mean(centred * centred, axis=-1, keepdims=True) + EPS)
    hat = centred * inverse
    normed = (hat * input_norm_gain).astype(jnp.bfloat16)

    def own_columns(array, index, axis):
        return lax.dynamic_slice_in_dim(array, index * width, width, axis)

    targets = [lax.rem(me + shift, parts) for shift in range(parts)]
    totals = [None] * parts
    start = 0
    for size, weight in zip(sizes, gathered):
        span = size * HD
        qkv = jnp.dot(
            normed, weight[:, : 3 * span], preferred_element_type=jnp.float32
        ).astype(jnp.bfloat16)
        upstream = jnp.dot(
            grads_full, weight[:, 3 * span :], preferred_element_type=jnp.float32
        ).astype(jnp.bfloat16)
        d_qkv = attention_grads(
            qkv, upstream, q_gain, k_gain, pattern[start : start + size]
        )
        for shift in range(parts):
            term = lax.dot_general(
                d_qkv,
                own_columns(weight, targets[shift], 0)[:, : 3 * span],
                (((1,), (1,)), ((), ())),
                preferred_element_type=jnp.float32,
            )
            totals[shift] = term if totals[shift] is None else totals[shift] + term
        start += size

    received = [exchange(totals[shift].astype(jnp.bfloat16), shift) for shift in range(1, parts)]
    sums = jnp.zeros((row_count, 2), jnp.float32)
    for shift in range(parts):
        gain = own_columns(input_norm_gain, targets[shift], 0)
        scaled = totals[shift] * gain
        sums = sums + jnp.stack(
            [
                jnp.sum(scaled, axis=-1),
                jnp.sum(scaled * own_columns(hat, targets[shift], 1), axis=-1),
            ],
            axis=1,
        )
    means = sums
    for shift in range(1, parts):
        means = means + exchange(sums, shift)
    means = means / (width * parts)
    d_normed = totals[0]
    for term in received:
        d_normed = d_normed + term.astype(jnp.float32)
    d_hat = d_normed * own_columns(input_norm_gain, me, 0)
    result = inverse * (d_hat - means[:, :1] - own_columns(hat, me, 1) * means[:, 1:])
    return result.astype(jnp.bfloat16)


def solution(mesh):
    return jax.shard_map(
        body,
        mesh=mesh,
        in_specs=(
            P("dp", "tensor"),
            P("dp", "tensor"),
            P(),
            P(),
            P(),
            P(None, "dp", "tensor"),
            P("tensor", "dp"),
            P("tensor", None, None),
        ),
        out_specs=P("dp", "tensor"),
        check_vma=False,
    )
```

time: 675 us -> 545 us (0.81)
  waiting for transfers between devices: 533 us -> 358 us
  Pallas kernels: 0 us -> 21.7 us
  matrix products: 80.3 us -> 95.9 us
    all_gather x4, waiting for transfers between devices: 445 us -> 268 us  [body(): gathered.append(lax.all_gather(piece, 'dp', axis=0, tiled=True))]
    ppermute x0 -> x4, waiting for transfers between devices: none -> 89.9 us  [exchange(): lax.ppermute(value, 'tensor', [(source, (source + shift) % parts) for sou...]
    psum x1 -> x0, waiting for transfers between devices: 85.8 us -> none  [body(): lax.psum(partial_grad.astype(jnp.bfloat16), 'tensor').astype(jnp.float32)]
    pallas_call x0 -> x4, Pallas kernels: none -> 21.7 us  [attention_grads(): pl.pallas_call(functools.partial(attention_kernel, heads, pattern.shape[2...]
    dot_general x8 -> x16, matrix products: 80.3 us -> 95.9 us  [the longest x4 38.2 us: body(): jnp.dot(normed, weight[:, :3 * span], preferred_element_type=jnp.float32)]
    another operation x4 -> x2, local copies, waits for them, and re-layouts: 13.1 us -> 2.35 us  [the longest x1 6.99 us: attend(): weights = jnp.exp(scores) * allowed[None]]
    dynamic_update_slice x0 -> x4, local copies, waits for them, and re-layouts: none -> 8.58 us  [the longest x2 4.32 us: whole_rows(): full = lax.dynamic_update_slice_in_dim(full, own, me * width, 1)]
    unnamed x26 -> x40, local copies, waits for them, and re-layouts: 1.8 us -> 10.3 us
  transfers between devices with their start and end apart: 5 -> 8, of which waited for: 5 -> 6; matrix products, arithmetic and copies ran while one was open for 4% -> 16% of each run, Pallas kernels for 0% -> 3%
where the time goes in v1:
time: 545 us; the launch traced here: 541 us
  waiting for transfers between devices  358 us (66%)
  matrix products  95.9 us (18%)
  local copies, waits for them, and re-layouts  32.9 us (6%)
  Pallas kernels  21.7 us (4%)
  other arithmetic  13.8 us (3%)
  between operations  13.8 us (3%)
  starting transfers between devices  5.52 us (1%)
    all_gather x4, waiting for transfers between devices, body(): gathered.append(lax.all_gather(piece, 'dp', axis=0, tiled=True))  268 us
    ppermute x4, waiting for transfers between devices, exchange(): lax.ppermute(value, 'tensor', [(source, (source + shift) % parts) for sou...  89.9 us
    dot_general x4, matrix products, body(): jnp.dot(normed, weight[:, :3 * span], preferred_element_type=jnp.float32)  38.2 us
    dot_general x8, matrix products, body(): lax.dot_general(d_qkv, own_columns(weight, targets[shift], 0)[:, :3 * spa...  35.2 us
    dot_general x4, matrix products, body(): jnp.dot(grads_full, weight[:, 3 * span:], preferred_element_type=jnp.floa...  22.5 us
    pallas_call x4, Pallas kernels, attention_grads(): pl.pallas_call(functools.partial(attention_kernel, heads, pattern.shape[2...  21.7 us
  transfers between devices with their start and end apart: 8, of which 6 were waited for; matrix products, arithmetic and copies ran while one was open for 16% of the time, Pallas kernels for 3%

profile of v1, /device:TPU:0, one launch (start us, length us, event | category | flops | bytes accessed | tf_op | source)
XLA Modules:
  0.0 541.4 jit_solution(7901364629380460905)
XLA Ops:
  6.5 1.0 fusion.77
  9.7 1.7 slice.158
  11.4 2.3 fusion.78
  13.7 1.9 copy.46
  15.6 1.8 copy.47
  17.4 1.8 copy.45
  19.3 2.5 pad_maximum_fusion.2
  21.8 1.4 fusion.79
  23.2 1.2 copy.42
  24.4 1.2 copy.43
  25.6 1.2 copy.44
  26.9 1.2 fusion.80
  28.1 1.3 pad_maximum_fusion.1
  30.4 1.3 pad_maximum_fusion
  31.7 3.0 collective-permute-start
  35.2 1.6 constant_dynamic-update-slice_fusion.3
  36.8 2.0 broadcast.31.clone.1
  38.8 2.7 constant_dynamic-update-slice_fusion.1
  44.7 25.6 %collective-permute-done = bf16[256,3072]{1,0:T(8,128)(2,1)} collective-permute-done((bf16[256,3072]{1,0:T(8,128)(2,1)}, bf16[256,3072]{1,0:T(8,128)(2,1)}, u32[]{:S(2)}, u32[]{:S(2)}) %collective-permute-start) | collective-permute-done | bytes 1572896 | tf_op jit(solution)/shard_map/ppermute | solution.py:128
  70.3 1.6 constant_dynamic-update-slice_fusion.2
  73.3 29.8 %collective-permute-done.1 = bf16[256,3072]{1,0:T(8,128)(2,1)} collective-permute-done((bf16[256,3072]{1,0:T(8,128)(2,1)}, bf16[256,3072]{1,0:T(8,128)(2,1)}, u32[]{:S(2)}, u32[]{:S(2)}) %collective-permute-start.1) | collective-permute-done | bytes 1572896 | tf_op jit(solution)/shard_map/ppermute | solution.py:128
  103.1 2.7 constant_dynamic-update-slice_fusion
  105.8 3.9 fusion.14
  109.7 4.1 fusion.66.up_ref
  113.8 4.8 fusion.63.qkv_ref
  118.7 2.9 shard_map.85
  121.6 55.3 %all-gather.9.cloned.1.call-done = bf16[6144,1536]{0,1:T(8,128)(2,1)} async-done(((bf16[384,1536]{0,1:T(8,128)(2,1)}), bf16[6144,1536]{0,1:T(8,128)(2,1)}) %all-gather.9.cloned.1.call-update) | async-done | bytes 18874384 | tf_op jit(solution)/shard_map/all_gather | solution.py:124
  176.9 5.8 %fusion.60.up_ref = bf16[256,384]{1,0:T(8,128)(2,1)} fusion(bf16[256,6144]{1,0:T(8,128)(2,1)} %constant_dynamic-update-slice_fusion, bf16[6144,1536]{0,1:T(8,128)(2,1)} %all-gather.9.cloned.1.call-done), kind=kOutput, calls=%fused_computation.55 | convolution fusion | flops 1208057856 | bytes 8060928 | tf_op jit(solution)/shard_map/dot_general | solution.py:160
  182.6 11.8 %fusion.41.qkv_ref = bf16[256,1152]{1,0:T(8,128)(2,1)} fusion(bf16[6144,1536]{0,1:T(8,128)(2,1)} %all-gather.9.cloned.1.call-done, f32[6144]{0:T(1024)S(1)} %copy-done.6, f32[256]{0:T(256)S(1)} %add_rsqrt_fusion, f32[256]{0:T(256)S(1)} %broadcast_multiply_fusion, bf16[256,6144]{1,0:T(8,128)(2,1)S(1)} %constant_dynamic-update-slice_fusion.2), kind=kOutput, calls=%fused_computation.43 | convolution fusion | flops 3632037888 | bytes 17917952 | tf_op jit(solution)/shard_map/dot_general | solution.py:157
  194.4 5.4 %shard_map.84 = bf16[256,1152]{1,0:T(8,128)(2,1)} custom-call(s32[24]{0:T(128)} %reshape.44.pattern_ref, f32[1,128]{1,0:T(1,128)} %bitcast.63, f32[1,128]{1,0:T(1,128)} %bitcast.67, bf16[256,1152]{1,0:T(8,128)(2,1)} %fusion.41.qkv_ref, bf16[256,384]{1,0:T(8,128)(2,1)} %fusion.60.up_ref), custom_call_target="tpu_custom_call" | custom-call | flops 503316480 | bytes 1376256 | tf_op jit(solution)/shard_map/pallas_call | solution.py:79
  199.9 107.0 %all-gather.7.cloned.1.call-done = bf16[6144,2048]{0,1:T(8,128)(2,1)} async-done(((bf16[384,2048]{0,1:T(8,128)(2,1)}), bf16[6144,2048]{0,1:T(8,128)(2,1)}) %all-gather.7.cloned.1.call-update) | async-done | bytes 25165840 | tf_op jit(solution)/shard_map/all_gather | solution.py:124
  306.8 6.3 %fusion.57.up_ref = bf16[256,512]{1,0:T(8,128)(2,1)} fusion(bf16[256,6144]{1,0:T(8,128)(2,1)} %constant_dynamic-update-slice_fusion, bf16[6144,2048]{0,1:T(8,128)(2,1)} %all-gather.7.cloned.1.call-done), kind=kOutput, calls=%fused_computation.53 | convolution fusion | flops 1610743808 | bytes 9699328 | tf_op jit(solution)/shard_map/dot_general | solution.py:160
  313.1 11.2 %fusion.47.qkv_ref = bf16[256,1536]{1,0:T(8,128)(2,1)} fusion(bf16[6144,2048]{0,1:T(8,128)(2,1)} %all-gather.7.cloned.1.call-done, f32[6144]{0:T(1024)S(1)} %copy-done.6, f32[256]{0:T(256)S(1)} %add_rsqrt_fusion, f32[256]{0:T(256)S(1)} %broadcast_multiply_fusion, bf16[256,6144]{1,0:T(8,128)(2,1)S(1)} %constant_dynamic-update-slice_fusion.2), kind=kOutput, calls=%fused_computation.45 | convolution fusion | flops 4840095744 | bytes 22833152 | tf_op jit(solution)/shard_map/dot_general | solution.py:157
  324.3 6.7 %shard_map.83 = bf16[256,1536]{1,0:T(8,128)(2,1)} custom-call(s32[32]{0:T(128)} %reshape.43.pattern_ref, f32[1,128]{1,0:T(1,128)} %bitcast.64, f32[1,128]{1,0:T(1,128)} %bitcast.68, bf16[256,1536]{1,0:T(8,128)(2,1)} %fusion.47.qkv_ref, bf16[256,512]{1,0:T(8,128)(2,1)} %fusion.57.up_ref), custom_call_target="tpu_custom_call" | custom-call | flops 671088640 | bytes 1835008 | tf_op jit(solution)/shard_map/pallas_call | solution.py:79
  331.0 105.7 %all-gather.5.cloned.1.call-done = bf16[6144,2048]{0,1:T(8,128)(2,1)} async-done(((bf16[384,2048]{0,1:T(8,128)(2,1)}), bf16[6144,2048]{0,1:T(8,128)(2,1)}) %all-gather.5.cloned.1.call-update) | async-done | bytes 25165840 | tf_op jit(solution)/shard_map/all_gather | solution.py:124
  436.7 10.3 %fusion.44.qkv_ref = bf16[256,1536]{1,0:T(8,128)(2,1)} fusion(bf16[6144,2048]{0,1:T(8,128)(2,1)} %all-gather.5.cloned.1.call-done, f32[6144]{0:T(1024)S(1)} %copy-done.6, f32[256]{0:T(256)S(1)} %add_rsqrt_fusion, f32[256]{0:T(256)S(1)} %broadcast_multiply_fusion, bf16[256,6144]{1,0:T(8,128)(2,1)S(1)} %constant_dynamic-update-slice_fusion.2), kind=kOutput, calls=%fused_computation.44 | convolution fusion | flops 4840095744 | bytes 22833152 | tf_op jit(solution)/shard_map/dot_general | solution.py:157
  447.0 6.3 %fusion.54.up_ref = bf16[256,512]{1,0:T(8,128)(2,1)} fusion(bf16[256,6144]{1,0:T(8,128)(2,1)} %constant_dynamic-update-slice_fusion, bf16[6144,2048]{0,1:T(8,128)(2,1)} %all-gather.5.cloned.1.call-done), kind=kOutput, calls=%fused_computation.52 | convolution fusion | flops 1610743808 | bytes 9699328 | tf_op jit(solution)/shard_map/dot_general | solution.py:160
  453.3 6.6 %shard_map.82 = bf16[256,1536]{1,0:T(8,128)(2,1)} custom-call(s32[32]{0:T(128)} %reshape.40.pattern_ref, f32[1,128]{1,0:T(1,128)} %bitcast.65, f32[1,128]{1,0:T(1,128)} %bitcast.69, bf16[256,1536]{1,0:T(8,128)(2,1)} %fusion.44.qkv_ref, bf16[256,512]{1,0:T(8,128)(2,1)} %fusion.54.up_ref), custom_call_target="tpu_custom_call" | custom-call | flops 671088640 | bytes 1835008 | tf_op jit(solution)/shard_map/pallas_call | solution.py:79
  460.0 5.2 fusion.6
  465.2 5.3 fusion.10
  470.5 5.2 fusion.38
  475.7 5.5 %fusion.35 = f32[256,3072]{1,0:T(8,128)S(1)} fusion(f32[256,3072]{1,0:T(8,128)S(1)} %fusion.10, bf16[256,1536]{1,0:T(8,128)(2,1)S(1)} %copy-done.9, bf16[6144,2048]{0,1:T(8,128)(2,1)} %all-gather.5.cloned.1.call-done, s32[]{:T(128)S(6)} %select_n.8), kind=kOutput, calls=%fused_computation.36 | convolution fusion | flops 2416705536 | bytes 16515076 | tf_op jit(solution)/shard_map/dot_general | solution.py:167
  481.3 5.6 %fusion.32 = f32[256,3072]{1,0:T(8,128)S(1)} fusion(f32[256,3072]{1,0:T(8,128)S(1)} %fusion.38, bf16[256,1152]{1,0:T(8,128)(2,1)S(1)} %copy-done.7, bf16[6144,1536]{0,1:T(8,128)(2,1)} %all-gather.9.cloned.1.call-done, s32[]{:T(128)S(6)} %select_n.7), kind=kOutput, calls=%fused_computation.35 | convolution fusion | flops 1812725760 | bytes 13959172 | tf_op jit(solution)/shard_map/dot_general | solution.py:167
  486.9 5.6 %fusion.29 = f32[256,3072]{1,0:T(8,128)S(1)} fusion(f32[256,3072]{1,0:T(8,128)S(1)} %fusion.35, bf16[256,1152]{1,0:T(8,128)(2,1)S(1)} %copy-done.7, bf16[6144,1536]{0,1:T(8,128)(2,1)} %all-gather.9.cloned.1.call-done, s32[]{:T(128)S(6)} %select_n.8), kind=kOutput, calls=%fused_computation.34 | convolution fusion | flops 1812725760 | bytes 13959172 | tf_op jit(solution)/shard_map/dot_general | solution.py:167
  493.5 1.9 multiply_reduce_fusion
  495.4 1.5 collective-permute-start.2
  497.6 34.5 %collective-permute-done.3 = f32[256,2]{0,1:T(2,128)S(1)} collective-permute-done((f32[256,2]{0,1:T(2,128)S(1)}, f32[256,2]{0,1:T(2,128)S(1)}, u32[]{:S(2)}, u32[]{:S(2)}) %collective-permute-start.3) | collective-permute-done | bytes 2080 | tf_op jit(solution)/shard_map/ppermute | solution.py:128
  532.1 2.5 multiply_convert_fusion.1
  (70 shorter events, 9.9 us)
Async XLA Ops:
  6.5 103.2 %all-gather.11.cloned.1.call-start = ((), (), s32[]{:S(2)}) async-start(), calls=%async_computation.3 | async-start | bytes 6684672 | tf_op jit(solution)/shard_map/all_gather | solution.py:124
  9.7 167.2 %all-gather.9.cloned.1.call-start = ((), (), s32[]{:S(2)}) async-start(), calls=%async_computation.2 | async-start | bytes 20054016 | tf_op jit(solution)/shard_map/all_gather | solution.py:124
  11.4 10.4 %copy-start = (bf16[3,384,1536]{2,1,0:T(8,128)(2,1)S(1)}, bf16[3,384,1536]{2,1,0:T(8,128)(2,1)}, u32[]{:S(2)}) copy-start(bf16[3,384,1536]{2,1,0:T(8,128)(2,1)} %param.13) | copy-start | bytes 10616836
  21.7 285.1 %all-gather.7.cloned.1.call-start = ((), (), s32[]{:S(2)}) async-start(), calls=%async_computation.1 | async-start | bytes 26738688 | tf_op jit(solution)/shard_map/all_gather | solution.py:124
  26.9 2.8 copy-start.3
  28.1 1.8 copy-start.2
  28.1 2.0 copy-start.1
  29.5 407.2 %all-gather.5.cloned.1.call-start = ((), (), s32[]{:S(2)}) async-start(), calls=%async_computation | async-start | bytes 26738688 | tf_op jit(solution)/shard_map/all_gather | solution.py:124
  29.9 4.9 copy-start.5
  31.7 38.5 %collective-permute-start = (bf16[256,3072]{1,0:T(8,128)(2,1)}, bf16[256,3072]{1,0:T(8,128)(2,1)}, u32[]{:S(2)}, u32[]{:S(2)}) collective-permute-start(bf16[256,3072]{1,0:T(8,128)(2,1)} %param.8), channel_id=1, source_target_pairs={{0,1},{1,0},{2,3},{3,2},{4,5},{5,4},{6,7},{7,6},{8,9},{9,8},{10,11... | collective-permute-start | bytes 4718600 | tf_op jit(solution)/shard_map/ppermute | solution.py:128
  34.7 68.4 %collective-permute-start.1 = (bf16[256,3072]{1,0:T(8,128)(2,1)}, bf16[256,3072]{1,0:T(8,128)(2,1)}, u32[]{:S(2)}, u32[]{:S(2)}) collective-permute-start(bf16[256,3072]{1,0:T(8,128)(2,1)} %param.9), channel_id=1, source_target_pairs={{0,1},{1,0},{2,3},{3,2},{4,5},{5,4},{6,7},{7,6},{8,9},{9,8},{10,11... | collective-permute-start | bytes 4718600 | tf_op jit(solution)/shard_map/ppermute | solution.py:128
  36.8 7.9 %copy-start.6 = (f32[6144]{0:T(1024)S(1)}, f32[6144]{0:T(1024)}, u32[]{:S(2)}) copy-start(f32[6144]{0:T(1024)} %param.10) | copy-start | bytes 73732
  447.0 13.0 %copy-start.8 = (bf16[256,1536]{1,0:T(8,128)(2,1)S(1)}, bf16[256,1536]{1,0:T(8,128)(2,1)}, u32[]{:S(2)}) copy-start(bf16[256,1536]{1,0:T(8,128)(2,1)} %shard_map.83) | copy-start | bytes 2359300
  465.2 5.3 copy-start.9
  475.7 5.6 %copy-start.7 = (bf16[256,1152]{1,0:T(8,128)(2,1)S(1)}, bf16[256,1152]{1,0:T(8,128)(2,1)}, u32[]{:S(2)}) copy-start(bf16[256,1152]{1,0:T(8,128)(2,1)} %shard_map.84) | copy-start | bytes 1769476
  475.7 16.8 %slice-start.2 = ((s8[6291456]{0:T(1024)(128)(4,1)}), s8[4194304]{0:T(1024)(128)(4,1)S(1)}, s32[]{:S(2)}) async-start(s8[6291456]{0:T(1024)(128)(4,1)} %bitcast.35), calls=%async_computation.6 | async-start | bytes 8388608
  481.3 11.2 %slice-start.3 = ((s8[6291456]{0:T(1024)(128)(4,1)}), s8[2097152]{0:T(1024)(128)(4,1)S(1)}, s32[]{:S(2)}) async-start(s8[6291456]{0:T(1024)(128)(4,1)} %bitcast.35), calls=%async_computation.7 | async-start | bytes 4194304
  481.3 12.2 %slice-start = ((s8[6291456]{0:T(1024)(128)(4,1)}), s8[4194304]{0:T(1024)(128)(4,1)S(1)}, s32[]{:S(2)}) async-start(s8[6291456]{0:T(1024)(128)(4,1)} %bitcast.33), calls=%async_computation.4 | async-start | bytes 8388608
  486.9 5.6 %copy-start.4 = (bf16[256,384]{1,0:T(8,128)(2,1)S(1)}, bf16[256,384]{1,0:T(8,128)(2,1)}, u32[]{:S(2)}) copy-start(bf16[256,384]{1,0:T(8,128)(2,1)} %shard_map.85) | copy-start | bytes 589828
  486.9 6.6 %slice-start.1 = ((s8[6291456]{0:T(1024)(128)(4,1)}), s8[2097152]{0:T(1024)(128)(4,1)S(1)}, s32[]{:S(2)}) async-start(s8[6291456]{0:T(1024)(128)(4,1)} %bitcast.33), calls=%async_computation.5 | async-start | bytes 4194304
  495.4 36.7 %collective-permute-start.2 = (bf16[256,3072]{1,0:T(8,128)(2,1)S(1)}, bf16[256,3072]{1,0:T(8,128)(2,1)S(1)}, u32[]{:S(2)}, u32[]{:S(2)}) collective-permute-start(bf16[256,3072]{1,0:T(8,128)(2,1)S(1)} %get-tuple-element.21), channel_id=1, source_target_pairs={{0,1},{1,0},{2,3},{3,2},{4,5},{5,4},{6,7},{7,6},{8,9},{9,8},{10,11... | collective-permute-start | bytes 4718600 | tf_op jit(solution)/shard_map/ppermute | solution.py:128
  497.0 35.1 %collective-permute-start.3 = (f32[256,2]{0,1:T(2,128)S(1)}, f32[256,2]{0,1:T(2,128)S(1)}, u32[]{:S(2)}, u32[]{:S(2)}) collective-permute-start(f32[256,2]{0,1:T(2,128)S(1)} %maximum_add_fusion), channel_id=1, source_target_pairs={{0,1},{1,0},{2,3},{3,2},{4,5},{5,4},{6,7},{7,6},{8,9},{9,8},{10,11... | collective-permute-start | bytes 6152 | tf_op jit(solution)/shard_map/ppermute | solution.py:128
Sparse Core Ops, SparseCore 0:
  9.8 69.2 all-gather.10
  80.6 96.1 all-gather.8
  178.4 128.3 all-gather.6
  308.2 128.3 all-gather.4

commit v2 on v1

--- a/solution.py
+++ b/solution.py
@@ -96,6 +96,26 @@
     )(pattern.reshape(-1), q_gain.reshape(1, HD), k_gain.reshape(1, HD), qkv, upstream)
 
 
+def piece_kernel(qkv_ref, out_ref, piece_ref):
+    width = qkv_ref.shape[2]
+    for part in range(3):
+        piece_ref[:, part * width : (part + 1) * width] = qkv_ref[part]
+    piece_ref[:, 3 * width :] = out_ref[...].T
+
+
+def weight_piece(w_qkv, w_out, start, size):
+    depth = w_qkv.shape[1]
+    width = size * HD
+    cols = slice(start * HD, start * HD + width)
+    return pl.pallas_call(
+        piece_kernel,
+        out_shape=jax.ShapeDtypeStruct((depth, 4 * width), w_qkv.dtype),
+        cost_estimate=pl.CostEstimate(
+            flops=0, bytes_accessed=16 * depth * width, transcendentals=0
+        ),
+    )(w_qkv[:, :, cols], w_out[cols])
+
+
 def head_chunks(heads):
     sizes = []
     left = heads - 1
@@ -112,15 +132,12 @@
     me = lax.axis_index("tensor")
     local_heads = w_qkv.shape[2] // HD
 
-    w_out_t = w_out.T
     gathered = []
     start = 0
     sizes = head_chunks(local_heads)
     for size in sizes:
-        cols = slice(start * HD, (start + size) * HD)
-        piece = jnp.concatenate(
-            [w_qkv[0, :, cols], w_qkv[1, :, cols], w_qkv[2, :, cols], w_out_t[:, cols]], axis=1
-        )
+        piece = weight_piece(w_qkv, w_out, start, size)
+        w_qkv, w_out, piece = lax.optimization_barrier((w_qkv, w_out, piece))
         gathered.append(lax.all_gather(piece, "dp", axis=0, tiled=True))
         start += size
 
@@ -145,6 +162,7 @@
     inverse = lax.rsqrt(jnp.mean(centred * centred, axis=-1, keepdims=True) + EPS)
     hat = centred * inverse
     normed = (hat * input_norm_gain).astype(jnp.bfloat16)
+    normed, grads_full = lax.optimization_barrier((normed, grads_full))
 
     def own_columns(array, index, axis):
         return lax.dynamic_slice_in_dim(array, index * width, width, axis)
@@ -163,7 +181,7 @@
         d_qkv = attention_grads(
             qkv, upstream, q_gain, k_gain, pattern[start : start + size]
         )
-        for shift in range(parts):
+        for shift in [*range(1, parts), 0]:
             term = lax.dot_general(
                 d_qkv,
                 own_columns(weight, targets[shift], 0)[:, : 3 * span],
@@ -172,6 +190,8 @@
             )
             totals[shift] = term if totals[shift] is None else totals[shift] + term
         start += size
+        if start < local_heads:
+            normed, grads_full, totals = lax.optimization_barrier((normed, grads_full, totals))
 
     received = [exchange(totals[shift].astype(jnp.bfloat16), shift) for shift in range(1, parts)]
     sums = jnp.zeros((row_count, 2), jnp.float32)

time: 545 us -> 511 us (0.938)
  waiting for transfers between devices: 358 us -> 313 us
  matrix products: 95.9 us -> 111 us
  local copies, waits for them, and re-layouts: 32.9 us -> 21.8 us
  Pallas kernels: 21.7 us -> 31.7 us
    all_gather x4, waiting for transfers between devices: 268 us -> 221 us  [body(): gathered.append(lax.all_gather(piece, 'dp', axis=0, tiled=True))]
    dot_general x8, matrix products: 35.2 us -> 56.6 us  [body(): lax.dot_general(d_qkv, own_columns(weight, targets[shift], 0)[:, :3 * spa...]
    pallas_call x0 -> x4, Pallas kernels: none -> 10 us  [weight_piece(): pl.pallas_call(piece_kernel, out_shape=jax.ShapeDtypeStruct((depth, 4 * w...]
    unnamed x40 -> x42, local copies, waits for them, and re-layouts: 10.3 us -> 2.21 us
    concatenate x4 -> x0, other arithmetic: 5.85 us -> none  [body(): jnp.concatenate([w_qkv[0, :, cols], w_qkv[1, :, cols], w_qkv[2, :, cols],...]
    slice x6 -> x8, local copies, waits for them, and re-layouts: 8.56 us -> 12.2 us  [the longest x4 6.97 us: weight_piece(): w_out[cols]]
  transfers between devices with their start and end apart: 8 -> 8, of which waited for: 6 -> 7; matrix products, arithmetic and copies ran while one was open for 16% -> 23% of each run, Pallas kernels for 3% -> 5%
where the time goes in v2:
time: 511 us; the launch traced here: 506 us
  waiting for transfers between devices  313 us (61%)
  matrix products  111 us (22%)
  Pallas kernels  31.7 us (6%)
  local copies, waits for them, and re-layouts  21.8 us (4%)
  between operations  13.8 us (3%)
  other arithmetic  9.22 us (2%)
  starting transfers between devices  5.17 us (1%)
    all_gather x4, waiting for transfers between devices, body(): gathered.append(lax.all_gather(piece, 'dp', axis=0, tiled=True))  221 us
    ppermute x4, waiting for transfers between devices, exchange(): lax.ppermute(value, 'tensor', [(source, (source + shift) % parts) for sou...  92.5 us
    dot_general x8, matrix products, body(): lax.dot_general(d_qkv, own_columns(weight, targets[shift], 0)[:, :3 * spa...  56.6 us
    dot_general x4, matrix products, body(): jnp.dot(normed, weight[:, :3 * span], preferred_element_type=jnp.float32)  35 us
    pallas_call x4, Pallas kernels, attention_grads(): pl.pallas_call(functools.partial(attention_kernel, heads, pattern.shape[2...  21.7 us
    dot_general x4, matrix products, body(): jnp.dot(grads_full, weight[:, 3 * span:], preferred_element_type=jnp.floa...  19 us
  transfers between devices with their start and end apart: 8, of which 7 were waited for; matrix products, arithmetic and copies ran while one was open for 23% of the time, Pallas kernels for 5%

profile of v2, /device:TPU:0, one launch (start us, length us, event | category | flops | bytes accessed | tf_op | source)
XLA Modules:
  0.0 505.5 jit_solution(15463161300331626487)
XLA Ops:
  6.5 2.4 slice.91.qkv_ref
  8.9 1.9 slice.92.out_ref
  10.8 2.7 shard_map.82
  13.6 1.1 slice.98.qkv_ref
  14.7 1.8 slice.99.out_ref
  16.5 2.7 shard_map.84
  19.2 1.0 slice.105.qkv_ref
  20.3 1.7 slice.106.out_ref
  22.0 2.8 shard_map.86
  24.9 2.8 collective-permute-start.1
  27.8 0.8 slice.112.qkv_ref
  28.6 1.5 slice.113.out_ref
  30.1 1.8 shard_map.88
  35.2 0.9 fusion.77
  37.2 0.9 copy-done.9
  38.2 25.0 %collective-permute-done.1 = bf16[256,3072]{1,0:T(8,128)(2,1)} collective-permute-done((bf16[256,3072]{1,0:T(8,128)(2,1)}, bf16[256,3072]{1,0:T(8,128)(2,1)}, u32[]{:S(2)}, u32[]{:S(2)}) %collective-permute-start.1) | collective-permute-done | bytes 1572896 | tf_op jit(solution)/shard_map/ppermute | solution.py:145
  63.2 33.0 %collective-permute-done = bf16[256,3072]{1,0:T(8,128)(2,1)} collective-permute-done((bf16[256,3072]{1,0:T(8,128)(2,1)}, bf16[256,3072]{1,0:T(8,128)(2,1)}, u32[]{:S(2)}, u32[]{:S(2)}) %collective-permute-start) | collective-permute-done | bytes 1572896 | tf_op jit(solution)/shard_map/ppermute | solution.py:145
  96.2 2.2 constant_dynamic-update-slice_fusion
  99.0 1.0 fusion.20
  100.0 5.3 %multiply_convert_fusion = (bf16[256,6144]{1,0:T(8,128)(2,1)}, f32[256,6144]{1,0:T(8,128)}) fusion(f32[6144]{0:T(1024)S(1)} %copy-done.11, f32[256]{0:T(256)S(1)} %add_rsqrt_fusion, f32[256]{0:T(256)S(1)} %broadcast_multiply_fusion, bf16[256,6144]{1,0:T(8,128)(2,1)S(1)} %get-tuple-element.69), kind=kLoop, calls=%fused_computation.27 | loop fusion | flops 7864320 | bytes 12609536 | tf_op jit(solution)/shard_map/convert_element_type | solution.py:164
  105.3 39.7 %all-gather.5.cloned.1.call-done = bf16[6144,2048]{1,0:T(8,128)(2,1)} async-done(((bf16[384,2048]{1,0:T(8,128)(2,1)}), bf16[6144,2048]{1,0:T(8,128)(2,1)}) %all-gather.5.cloned.1.call-update) | async-done | bytes 25165840 | tf_op jit(solution)/shard_map/all_gather | solution.py:141
  145.0 5.4 %fusion.54.up_ref = bf16[256,512]{1,0:T(8,128)(2,1)} fusion(bf16[256,6144]{1,0:T(8,128)(2,1)S(1)} %get-tuple-element.51, bf16[6144,2048]{1,0:T(8,128)(2,1)} %all-gather.5.cloned.1.call-done), kind=kOutput, calls=%fused_computation.50 | convolution fusion | flops 1610743808 | bytes 9699328 | tf_op jit(solution)/shard_map/dot_general | solution.py:178
  150.4 10.7 %fusion.44.qkv_ref = bf16[256,1536]{1,0:T(8,128)(2,1)} fusion(bf16[256,6144]{1,0:T(8,128)(2,1)S(1)} %copy-done.4, bf16[6144,2048]{1,0:T(8,128)(2,1)} %all-gather.5.cloned.1.call-done), kind=kOutput, calls=%fused_computation.44 | convolution fusion | flops 4832231424 | bytes 22806528 | tf_op jit(solution)/shard_map/dot_general | solution.py:175
  161.1 6.7 %shard_map.83 = bf16[256,1536]{1,0:T(8,128)(2,1)} custom-call(s32[32]{0:T(128)} %reshape.40.pattern_ref, f32[1,128]{1,0:T(1,128)} %bitcast.36, f32[1,128]{1,0:T(1,128)} %bitcast.40, bf16[256,1536]{1,0:T(8,128)(2,1)} %fusion.44.qkv_ref, bf16[256,512]{1,0:T(8,128)(2,1)} %fusion.54.up_ref), custom_call_target="tpu_custom_call" | custom-call | flops 671088640 | bytes 1835008 | tf_op jit(solution)/shard_map/pallas_call | solution.py:79
  167.8 8.6 %fusion.12 = f32[256,3072]{1,0:T(8,128)} fusion(bf16[256,1536]{1,0:T(8,128)(2,1)} %shard_map.83, bf16[6144,2048]{1,0:T(8,128)(2,1)} %all-gather.5.cloned.1.call-done, s32[]{:T(128)S(6)} %select_n.8), kind=kOutput, calls=%fused_computation.12 | convolution fusion | flops 2415919104 | bytes 13369348 | tf_op jit(solution)/shard_map/dot_general | solution.py:185
  176.4 8.3 %fusion.10 = f32[256,3072]{1,0:T(8,128)} fusion(bf16[256,1536]{1,0:T(8,128)(2,1)S(1)} %copy-done.15, bf16[6144,2048]{1,0:T(8,128)(2,1)} %all-gather.5.cloned.1.call-done, s32[]{:T(128)S(6)} %select_n.7), kind=kOutput, calls=%fused_computation.10 | convolution fusion | flops 2415919104 | bytes 13369348 | tf_op jit(solution)/shard_map/dot_general | solution.py:185
  184.6 90.6 %all-gather.7.cloned.1.call-done = bf16[6144,2048]{1,0:T(8,128)(2,1)} async-done(((bf16[384,2048]{1,0:T(8,128)(2,1)}), bf16[6144,2048]{1,0:T(8,128)(2,1)}) %all-gather.7.cloned.1.call-update) | async-done | bytes 25165840 | tf_op jit(solution)/shard_map/all_gather | solution.py:141
  275.2 5.4 %fusion.57.up_ref = bf16[256,512]{1,0:T(8,128)(2,1)} fusion(bf16[256,6144]{1,0:T(8,128)(2,1)S(1)} %get-tuple-element.51, bf16[6144,2048]{1,0:T(8,128)(2,1)} %all-gather.7.cloned.1.call-done), kind=kOutput, calls=%fused_computation.51 | convolution fusion | flops 1610743808 | bytes 9699328 | tf_op jit(solution)/shard_map/dot_general | solution.py:178
  280.6 10.6 %fusion.47.qkv_ref = bf16[256,1536]{1,0:T(8,128)(2,1)} fusion(bf16[256,6144]{1,0:T(8,128)(2,1)S(1)} %copy-done.5, bf16[6144,2048]{1,0:T(8,128)(2,1)} %all-gather.7.cloned.1.call-done), kind=kOutput, calls=%fused_computation.45 | convolution fusion | flops 4832231424 | bytes 22806528 | tf_op jit(solution)/shard_map/dot_general | solution.py:175
  291.2 6.7 %shard_map.85 = bf16[256,1536]{1,0:T(8,128)(2,1)} custom-call(s32[32]{0:T(128)} %reshape.43.pattern_ref, f32[1,128]{1,0:T(1,128)} %bitcast.37, f32[1,128]{1,0:T(1,128)} %bitcast.41, bf16[256,1536]{1,0:T(8,128)(2,1)} %fusion.47.qkv_ref, bf16[256,512]{1,0:T(8,128)(2,1)} %fusion.57.up_ref), custom_call_target="tpu_custom_call" | custom-call | flops 671088640 | bytes 1835008 | tf_op jit(solution)/shard_map/pallas_call | solution.py:79
  297.8 9.6 %fusion.35 = f32[256,3072]{1,0:T(8,128)} fusion(f32[256,3072]{1,0:T(8,128)} %fusion.12, bf16[256,1536]{1,0:T(8,128)(2,1)} %shard_map.85, bf16[6144,2048]{1,0:T(8,128)(2,1)} %all-gather.7.cloned.1.call-done, s32[]{:T(128)S(6)} %select_n.8), kind=kOutput, calls=%fused_computation.36 | convolution fusion | flops 2416705536 | bytes 16515076 | tf_op jit(solution)/shard_map/dot_general | solution.py:185
  307.4 8.2 %fusion.38 = f32[256,3072]{1,0:T(8,128)} fusion(f32[256,3072]{1,0:T(8,128)S(1)} %copy-done.18, bf16[256,1536]{1,0:T(8,128)(2,1)S(1)} %copy-done.14, bf16[6144,2048]{1,0:T(8,128)(2,1)} %all-gather.7.cloned.1.call-done, s32[]{:T(128)S(6)} %select_n.7), kind=kOutput, calls=%fused_computation.37 | convolution fusion | flops 2416705536 | bytes 16515076 | tf_op jit(solution)/shard_map/dot_general | solution.py:185
  315.6 60.1 %all-gather.9.cloned.1.call-done = bf16[6144,1536]{1,0:T(8,128)(2,1)} async-done(((bf16[384,1536]{1,0:T(8,128)(2,1)}), bf16[6144,1536]{1,0:T(8,128)(2,1)}) %all-gather.9.cloned.1.call-update) | async-done | bytes 18874384 | tf_op jit(solution)/shard_map/all_gather | solution.py:141
  375.8 5.0 fusion.60.up_ref
  380.8 8.8 %fusion.41.qkv_ref = bf16[256,1152]{1,0:T(8,128)(2,1)} fusion(bf16[256,6144]{1,0:T(8,128)(2,1)S(1)} %copy-done.6, bf16[6144,1536]{1,0:T(8,128)(2,1)} %all-gather.9.cloned.1.call-done), kind=kOutput, calls=%fused_computation.43 | convolution fusion | flops 3624173568 | bytes 17891328 | tf_op jit(solution)/shard_map/dot_general | solution.py:175
  389.5 5.4 %shard_map.87 = bf16[256,1152]{1,0:T(8,128)(2,1)} custom-call(s32[24]{0:T(128)} %reshape.44.pattern_ref, f32[1,128]{1,0:T(1,128)} %bitcast.38, f32[1,128]{1,0:T(1,128)} %bitcast.42, bf16[256,1152]{1,0:T(8,128)(2,1)} %fusion.41.qkv_ref, bf16[256,384]{1,0:T(8,128)(2,1)} %fusion.60.up_ref), custom_call_target="tpu_custom_call" | custom-call | flops 503316480 | bytes 1376256 | tf_op jit(solution)/shard_map/pallas_call | solution.py:79
  395.0 7.2 %fusion.29 = f32[256,3072]{1,0:T(8,128)} fusion(f32[256,3072]{1,0:T(8,128)S(1)} %copy-done.17, bf16[256,1152]{1,0:T(8,128)(2,1)} %shard_map.87, bf16[6144,1536]{1,0:T(8,128)(2,1)} %all-gather.9.cloned.1.call-done, s32[]{:T(128)S(6)} %select_n.8), kind=kOutput, calls=%fused_computation.34 | convolution fusion | flops 1812725760 | bytes 13959172 | tf_op jit(solution)/shard_map/dot_general | solution.py:185
  402.2 7.2 %fusion.32 = f32[256,3072]{1,0:T(8,128)} fusion(f32[256,3072]{1,0:T(8,128)S(1)} %copy-done.16, bf16[256,1152]{1,0:T(8,128)(2,1)S(1)} %copy-done.13, bf16[6144,1536]{1,0:T(8,128)(2,1)} %all-gather.9.cloned.1.call-done, s32[]{:T(128)S(6)} %select_n.7), kind=kOutput, calls=%fused_computation.35 | convolution fusion | flops 1812725760 | bytes 13959172 | tf_op jit(solution)/shard_map/dot_general | solution.py:185
  409.4 30.4 %all-gather.11.cloned.1.call-done = bf16[6144,512]{1,0:T(8,128)(2,1)} async-done(((bf16[384,512]{1,0:T(8,128)(2,1)}), bf16[6144,512]{1,0:T(8,128)(2,1)}) %all-gather.11.cloned.1.call-update) | async-done | bytes 6291472 | tf_op jit(solution)/shard_map/all_gather | solution.py:141
  439.8 5.0 fusion.63.qkv_ref
  444.7 3.2 fusion.66.up_ref
  447.9 2.9 shard_map.89
  450.9 3.8 convolution_add_fusion.1
  454.7 1.0 copy-done.1
  455.7 3.7 multiply_reduce_fusion
  459.4 1.5 collective-permute-start.2
  461.6 34.5 %collective-permute-done.3 = f32[256,2]{0,1:T(2,128)S(1)} collective-permute-done((f32[256,2]{0,1:T(2,128)S(1)}, f32[256,2]{0,1:T(2,128)S(1)}, u32[]{:S(2)}, u32[]{:S(2)}) %collective-permute-start.3) | collective-permute-done | bytes 2080 | tf_op jit(solution)/shard_map/ppermute | solution.py:145
  496.1 2.4 multiply_convert_fusion.1
  (72 shorter events, 6.0 us)
Async XLA Ops:
  6.5 138.5 %all-gather.5.cloned.1.call-start = ((), (), s32[]{:S(2)}) async-start(), calls=%async_computation | async-start | bytes 26738688 | tf_op jit(solution)/shard_map/all_gather | solution.py:141
  8.9 4.7 copy-start
  13.5 261.7 %all-gather.7.cloned.1.call-start = ((), (), s32[]{:S(2)}) async-start(), calls=%async_computation.1 | async-start | bytes 26738688 | tf_op jit(solution)/shard_map/all_gather | solution.py:141
  19.2 356.6 %all-gather.9.cloned.1.call-start = ((), (), s32[]{:S(2)}) async-start(), calls=%async_computation.2 | async-start | bytes 20054016 | tf_op jit(solution)/shard_map/all_gather | solution.py:141
  20.3 11.7 %copy-start.12 = (s32[12,4,2]{0,2,1:T(2,128)S(1)}, s32[12,4,2]{0,2,1:T(2,128)}, u32[]{:S(2)}) copy-start(s32[12,4,2]{0,2,1:T(2,128)} %param.15) | copy-start | bytes 1156
  24.8 414.9 %all-gather.11.cloned.1.call-start = ((), (), s32[]{:S(2)}) async-start(), calls=%async_computation.3 | async-start | bytes 6684672 | tf_op jit(solution)/shard_map/all_gather | solution.py:141
  24.9 38.3 %collective-permute-start.1 = (bf16[256,3072]{1,0:T(8,128)(2,1)}, bf16[256,3072]{1,0:T(8,128)(2,1)}, u32[]{:S(2)}, u32[]{:S(2)}) collective-permute-start(bf16[256,3072]{1,0:T(8,128)(2,1)} %param.9), channel_id=1, source_target_pairs={{0,1},{1,0},{2,3},{3,2},{4,5},{5,4},{6,7},{7,6},{8,9},{9,8},{10,11... | collective-permute-start | bytes 4718600 | tf_op jit(solution)/shard_map/ppermute | solution.py:145
  27.7 68.5 %collective-permute-start = (bf16[256,3072]{1,0:T(8,128)(2,1)}, bf16[256,3072]{1,0:T(8,128)(2,1)}, u32[]{:S(2)}, u32[]{:S(2)}) collective-permute-start(bf16[256,3072]{1,0:T(8,128)(2,1)} %param.8), channel_id=1, source_target_pairs={{0,1},{1,0},{2,3},{3,2},{4,5},{5,4},{6,7},{7,6},{8,9},{9,8},{10,11... | collective-permute-start | bytes 4718600 | tf_op jit(solution)/shard_map/ppermute | solution.py:145
  35.2 1.5 copy-start.8
  36.6 1.4 copy-start.9
  98.5 277.3 %copy-start.2 = (bf16[256,6144]{1,0:T(8,128)(2,1)}, bf16[256,6144]{1,0:T(8,128)(2,1)S(1)}, u32[]{:S(2)}) copy-start(bf16[256,6144]{1,0:T(8,128)(2,1)S(1)} %get-tuple-element.51) | copy-start | bytes 9437188
  98.5 1.5 copy-start.11
  145.0 5.4 %copy-start.4 = (bf16[256,6144]{1,0:T(8,128)(2,1)S(1)}, bf16[256,6144]{1,0:T(8,128)(2,1)}, u32[]{:S(2)}) copy-start(bf16[256,6144]{1,0:T(8,128)(2,1)} %get-tuple-element.47) | copy-start | bytes 9437188
  167.8 8.6 %copy-start.15 = (bf16[256,1536]{1,0:T(8,128)(2,1)S(1)}, bf16[256,1536]{1,0:T(8,128)(2,1)}, u32[]{:S(2)}) copy-start(bf16[256,1536]{1,0:T(8,128)(2,1)} %shard_map.83) | copy-start | bytes 2359300
  275.2 5.4 %copy-start.5 = (bf16[256,6144]{1,0:T(8,128)(2,1)S(1)}, bf16[256,6144]{1,0:T(8,128)(2,1)}, u32[]{:S(2)}) copy-start(bf16[256,6144]{1,0:T(8,128)(2,1)} %get-tuple-element.47) | copy-start | bytes 9437188
  297.8 9.6 %copy-start.14 = (bf16[256,1536]{1,0:T(8,128)(2,1)S(1)}, bf16[256,1536]{1,0:T(8,128)(2,1)}, u32[]{:S(2)}) copy-start(bf16[256,1536]{1,0:T(8,128)(2,1)} %shard_map.85) | copy-start | bytes 2359300
  297.8 9.6 %copy-start.18 = (f32[256,3072]{1,0:T(8,128)S(1)}, f32[256,3072]{1,0:T(8,128)}, u32[]{:S(2)}) copy-start(f32[256,3072]{1,0:T(8,128)} %fusion.10) | copy-start | bytes 9437188
  375.8 5.0 copy-start.6
  380.7 14.2 %copy-start.17 = (f32[256,3072]{1,0:T(8,128)S(1)}, f32[256,3072]{1,0:T(8,128)}, u32[]{:S(2)}) copy-start(f32[256,3072]{1,0:T(8,128)} %fusion.35) | copy-start | bytes 9437188
  395.0 7.2 %copy-start.13 = (bf16[256,1152]{1,0:T(8,128)(2,1)S(1)}, bf16[256,1152]{1,0:T(8,128)(2,1)}, u32[]{:S(2)}) copy-start(bf16[256,1152]{1,0:T(8,128)(2,1)} %shard_map.87) | copy-start | bytes 1769476
  395.0 7.2 %copy-start.16 = (f32[256,3072]{1,0:T(8,128)S(1)}, f32[256,3072]{1,0:T(8,128)}, u32[]{:S(2)}) copy-start(f32[256,3072]{1,0:T(8,128)} %fusion.38) | copy-start | bytes 9437188
  402.2 37.6 %copy-start.7 = (bf16[256,6144]{1,0:T(8,128)(2,1)S(1)}, bf16[256,6144]{1,0:T(8,128)(2,1)}, u32[]{:S(2)}) copy-start(bf16[256,6144]{1,0:T(8,128)(2,1)} %get-tuple-element.47) | copy-start | bytes 9437188
  439.8 5.0 copy-start.3
  444.7 10.0 %slice-start = ((s8[6291456]{0:T(1024)(128)(4,1)}), s8[2097152]{0:T(1024)(128)(4,1)S(1)}, s32[]{:S(2)}) async-start(s8[6291456]{0:T(1024)(128)(4,1)} %bitcast.24), calls=%async_computation.4 | async-start | bytes 4194304
  450.9 3.9 slice-start.1
  450.9 4.9 copy-start.1
  450.9 4.9 copy-start.10
  459.4 36.7 %collective-permute-start.2 = (bf16[256,3072]{1,0:T(8,128)(2,1)S(1)}, bf16[256,3072]{1,0:T(8,128)(2,1)S(1)}, u32[]{:S(2)}, u32[]{:S(2)}) collective-permute-start(bf16[256,3072]{1,0:T(8,128)(2,1)S(1)} %get-tuple-element.59), channel_id=1, source_target_pairs={{0,1},{1,0},{2,3},{3,2},{4,5},{5,4},{6,7},{7,6},{8,9},{9,8},{10,11... | collective-permute-start | bytes 4718600 | tf_op jit(solution)/shard_map/ppermute | solution.py:145
  460.9 35.1 %collective-permute-start.3 = (f32[256,2]{0,1:T(2,128)S(1)}, f32[256,2]{0,1:T(2,128)S(1)}, u32[]{:S(2)}, u32[]{:S(2)}) collective-permute-start(f32[256,2]{0,1:T(2,128)S(1)} %maximum_add_fusion), channel_id=1, source_target_pairs={{0,1},{1,0},{2,3},{3,2},{4,5},{5,4},{6,7},{7,6},{8,9},{9,8},{10,11... | collective-permute-start | bytes 6152 | tf_op jit(solution)/shard_map/ppermute | solution.py:145
Sparse Core Ops, SparseCore 0:
  13.7 131.2 all-gather.4
  146.6 128.5 all-gather.6
  276.8 98.9 all-gather.8
  377.9 61.8 all-gather.10

commit v3 on v2

--- a/solution.py
+++ b/solution.py
@@ -14,8 +14,8 @@
 EPS = 1e-06
 
 
-def attention_kernel(heads, ksel, pattern_ref, q_gain_ref, k_gain_ref, qkv_ref, up_ref, out_ref):
-    width = heads * HD
+def attention_kernel(ksel, pattern_ref, q_gain_ref, k_gain_ref, qkv_ref, up_ref, out_ref):
+    head = pl.program_id(1)
     scale = 1.0 / math.sqrt(HD)
     q_gain = q_gain_ref[...]
     k_gain = k_gain_ref[...]
@@ -40,36 +40,30 @@
             a, b, (dims, ((), ())), precision=precision, preferred_element_type=jnp.float32
         )
 
-    for head in range(heads):
-        lo = head * HD
-        q_hat, q_inverse = normalize(qkv_ref[:, lo : lo + HD].astype(jnp.float32))
-        k_hat, k_inverse = normalize(
-            qkv_ref[:, width + lo : width + lo + HD].astype(jnp.float32)
-        )
-        value = qkv_ref[:, 2 * width + lo : 2 * width + lo + HD]
-        upstream = up_ref[:, lo : lo + HD]
-        q_normed = q_hat * q_gain
-        k_normed = k_hat * k_gain
-        scores = dot(q_normed * scale, k_normed, ((1,), (1,)), lax.Precision.HIGHEST)
-        rows = []
-        for i in range(blocks):
-            hit = column_block == pattern_ref[(head * blocks + i) * ksel]
-            for s in range(1, ksel):
-                hit = hit | (column_block == pattern_ref[(head * blocks + i) * ksel + s])
-            rows.append(jnp.where(hit, jnp.exp(scores[i * BLK : (i + 1) * BLK]), 0.0))
-        weights = jnp.concatenate(rows, axis=0)
-        probs = weights / jnp.sum(weights, axis=-1, keepdims=True)
-        d_probs = dot(upstream, value, ((1,), (1,)))
-        d_value = dot(probs.astype(jnp.bfloat16), upstream, ((0,), (0,)))
-        d_scores = probs * (d_probs - jnp.sum(probs * d_probs, axis=-1, keepdims=True))
-        d_scores = (d_scores * scale).astype(jnp.bfloat16)
-        d_q = dot(d_scores, k_normed.astype(jnp.bfloat16), ((1,), (0,)))
-        d_k = dot(d_scores, q_normed.astype(jnp.bfloat16), ((0,), (0,)))
-        out_ref[:, lo : lo + HD] = pull_back(d_q, q_hat, q_inverse, q_gain).astype(jnp.bfloat16)
-        out_ref[:, width + lo : width + lo + HD] = pull_back(
-            d_k, k_hat, k_inverse, k_gain
-        ).astype(jnp.bfloat16)
-        out_ref[:, 2 * width + lo : 2 * width + lo + HD] = d_value.astype(jnp.bfloat16)
+    q_hat, q_inverse = normalize(qkv_ref[:, :HD].astype(jnp.float32))
+    k_hat, k_inverse = normalize(qkv_ref[:, HD : 2 * HD].astype(jnp.float32))
+    value = qkv_ref[:, 2 * HD :]
+    upstream = up_ref[...]
+    q_normed = q_hat * q_gain
+    k_normed = k_hat * k_gain
+    scores = dot(q_normed * scale, k_normed, ((1,), (1,)), lax.Precision.HIGHEST)
+    rows = []
+    for i in range(blocks):
+        hit = column_block == pattern_ref[(head * blocks + i) * ksel]
+        for s in range(1, ksel):
+            hit = hit | (column_block == pattern_ref[(head * blocks + i) * ksel + s])
+        rows.append(jnp.where(hit, jnp.exp(scores[i * BLK : (i + 1) * BLK]), 0.0))
+    weights = jnp.concatenate(rows, axis=0)
+    probs = weights / jnp.sum(weights, axis=-1, keepdims=True)
+    d_probs = dot(upstream, value, ((1,), (1,)))
+    d_value = dot(probs.astype(jnp.bfloat16), upstream, ((0,), (0,)))
+    d_scores = probs * (d_probs - jnp.sum(probs * d_probs, axis=-1, keepdims=True))
+    d_scores = (d_scores * scale).astype(jnp.bfloat16)
+    d_q = dot(d_scores, k_normed.astype(jnp.bfloat16), ((1,), (0,)))
+    d_k = dot(d_scores, q_normed.astype(jnp.bfloat16), ((0,), (0,)))
+    out_ref[:, :HD] = pull_back(d_q, q_hat, q_inverse, q_gain).astype(jnp.bfloat16)
+    out_ref[:, HD : 2 * HD] = pull_back(d_k, k_hat, k_inverse, k_gain).astype(jnp.bfloat16)
+    out_ref[:, 2 * HD :] = d_value.astype(jnp.bfloat16)
 
 
 def attention_grads(qkv, upstream, q_gain, k_gain, pattern):
@@ -77,17 +71,17 @@
     heads = width // HD
     images = rows // SEQ
     return pl.pallas_call(
-        functools.partial(attention_kernel, heads, pattern.shape[2]),
-        grid=(images,),
+        functools.partial(attention_kernel, pattern.shape[2]),
+        grid=(images, heads),
         out_shape=jax.ShapeDtypeStruct((rows, 3 * width), jnp.bfloat16),
         in_specs=[
             pl.BlockSpec(memory_space=pltpu.SMEM),
-            pl.BlockSpec((1, HD), lambda i: (0, 0)),
-            pl.BlockSpec((1, HD), lambda i: (0, 0)),
-            pl.BlockSpec((SEQ, 3 * width), lambda i: (i, 0)),
-            pl.BlockSpec((SEQ, width), lambda i: (i, 0)),
+            pl.BlockSpec((1, HD), lambda i, h: (0, 0)),
+            pl.BlockSpec((1, HD), lambda i, h: (0, 0)),
+            pl.BlockSpec((SEQ, 3 * HD), lambda i, h: (i, h)),
+            pl.BlockSpec((SEQ, HD), lambda i, h: (i, h)),
         ],
-        out_specs=pl.BlockSpec((SEQ, 3 * width), lambda i: (i, 0)),
+        out_specs=pl.BlockSpec((SEQ, 3 * HD), lambda i, h: (i, h)),
         cost_estimate=pl.CostEstimate(
             flops=images * heads * 20 * SEQ * SEQ * HD,
             bytes_accessed=rows * width * 14,
@@ -96,34 +90,42 @@
     )(pattern.reshape(-1), q_gain.reshape(1, HD), k_gain.reshape(1, HD), qkv, upstream)
 
 
-def piece_kernel(qkv_ref, out_ref, piece_ref):
-    width = qkv_ref.shape[2]
-    for part in range(3):
-        piece_ref[:, part * width : (part + 1) * width] = qkv_ref[part]
-    piece_ref[:, 3 * width :] = out_ref[...].T
-
-
-def weight_piece(w_qkv, w_out, start, size):
-    depth = w_qkv.shape[1]
-    width = size * HD
-    cols = slice(start * HD, start * HD + width)
+def piece_kernel(sizes, qkv_ref, out_ref, *piece_refs):
+    start = 0
+    for size, piece_ref in zip(sizes, piece_refs):
+        for head in range(size):
+            cols = slice((start + head) * HD, (start + head + 1) * HD)
+            for part in range(3):
+                lo = (3 * head + part) * HD
+                piece_ref[:, lo : lo + HD] = qkv_ref[part, :, cols]
+        cols = slice(start * HD, (start + size) * HD)
+        piece_ref[:, 3 * size * HD :] = out_ref[cols, :].T
+        start += size
+
+
+def weight_pieces(w_qkv, w_out, sizes):
+    depth, width = w_qkv.shape[1:]
+    step = HD if depth % HD == 0 else depth
     return pl.pallas_call(
-        piece_kernel,
-        out_shape=jax.ShapeDtypeStruct((depth, 4 * width), w_qkv.dtype),
+        functools.partial(piece_kernel, sizes),
+        grid=(depth // step,),
+        out_shape=[
+            jax.ShapeDtypeStruct((depth, 4 * size * HD), w_qkv.dtype) for size in sizes
+        ],
+        in_specs=[
+            pl.BlockSpec((3, step, width), lambda i: (0, i, 0)),
+            pl.BlockSpec((width, step), lambda i: (0, i)),
+        ],
+        out_specs=[pl.BlockSpec((step, 4 * size * HD), lambda i: (i, 0)) for size in sizes],
         cost_estimate=pl.CostEstimate(
             flops=0, bytes_accessed=16 * depth * width, transcendentals=0
         ),
-    )(w_qkv[:, :, cols], w_out[cols])
+    )(w_qkv, w_out)
 
 
 def head_chunks(heads):
-    sizes = []
-    left = heads - 1
-    while left > 0:
-        take = min(4, left)
-        sizes.append(take)
-        left -= take
-    return sizes + [1]
+    last = max(1, heads // 4)
+    return [size for size in (heads - last, last) if size > 0]
 
 
 def body(tokens, grad_out, input_norm_gain, q_gain, k_gain, w_qkv, w_out, pattern):
@@ -132,14 +134,9 @@
     me = lax.axis_index("tensor")
     local_heads = w_qkv.shape[2] // HD
 
-    gathered = []
-    start = 0
     sizes = head_chunks(local_heads)
-    for size in sizes:
-        piece = weight_piece(w_qkv, w_out, start, size)
-        w_qkv, w_out, piece = lax.optimization_barrier((w_qkv, w_out, piece))
-        gathered.append(lax.all_gather(piece, "dp", axis=0, tiled=True))
-        start += size
+    pieces = weight_pieces(w_qkv, w_out, sizes)
+    gathered = [lax.all_gather(piece, "dp", axis=0, tiled=True) for piece in pieces]
 
     def exchange(value, shift):
         return lax.ppermute(

time: 511 us -> 471 us (0.922); the launches traced: 506 us -> 471 us
  matrix products: 111 us -> 80.7 us
  waiting for transfers between devices: 313 us -> 330 us
  local copies, waits for them, and re-layouts: 21.8 us -> 7.85 us
  Pallas kernels: 31.7 us -> 24.4 us
    dot_general x8 -> x4, matrix products: 56.6 us -> 38.5 us  [body(): lax.dot_general(d_qkv, own_columns(weight, targets[shift], 0)[:, :3 * spa...]
    slice x8 -> x0, local copies, waits for them, and re-layouts: 12.2 us -> none  [the longest x4 6.97 us: weight_piece(): w_out[cols]]
    all_gather x4 -> x2, waiting for transfers between devices: 221 us -> 232 us  [body(): lax.all_gather(piece, 'dp', axis=0, tiled=True)]
    pallas_call x8 -> x3, Pallas kernels: 31.7 us -> 24.4 us  [the longest x2 18.9 us: attention_grads(): pl.pallas_call(functools.partial(attention_kernel, pattern.shape[2]), gri...]
    dot_general x4 -> x2, matrix products: 35 us -> 28.7 us  [body(): jnp.dot(normed, weight[:, :3 * span], preferred_element_type=jnp.float32)]
    dot_general x4 -> x2, matrix products: 19 us -> 13.5 us  [body(): jnp.dot(grads_full, weight[:, 3 * span:], preferred_element_type=jnp.floa...]
  transfers between devices with their start and end apart: 8 -> 6, of which waited for: 7 -> 5; matrix products, arithmetic and copies ran while one was open for 23% -> 15% of each run, Pallas kernels for 5% -> 3%
where the time goes in v3:
time: 471 us
  waiting for transfers between devices  330 us (70%)
  matrix products  80.7 us (17%)
  Pallas kernels  24.4 us (5%)
  between operations  13.5 us (3%)
  other arithmetic  9.24 us (2%)
  local copies, waits for them, and re-layouts  7.85 us (2%)
  starting transfers between devices  5.28 us (1%)
    all_gather x2, waiting for transfers between devices, body(): lax.all_gather(piece, 'dp', axis=0, tiled=True)  232 us
    ppermute x4, waiting for transfers between devices, exchange(): lax.ppermute(value, 'tensor', [(source, (source + shift) % parts) for sou...  97.3 us
    dot_general x4, matrix products, body(): lax.dot_general(d_qkv, own_columns(weight, targets[shift], 0)[:, :3 * spa...  38.5 us
    dot_general x2, matrix products, body(): jnp.dot(normed, weight[:, :3 * span], preferred_element_type=jnp.float32)  28.7 us
    pallas_call x2, Pallas kernels, attention_grads(): pl.pallas_call(functools.partial(attention_kernel, pattern.shape[2]), gri...  18.9 us
    dot_general x2, matrix products, body(): jnp.dot(grads_full, weight[:, 3 * span:], preferred_element_type=jnp.floa...  13.5 us
  transfers between devices with their start and end apart: 6, of which 5 were waited for; matrix products, arithmetic and copies ran while one was open for 15% of the time, Pallas kernels for 3%

profile of v3, /device:TPU:0, one launch (start us, length us, event | category | flops | bytes accessed | tf_op | source)
XLA Modules:
  0.0 470.7 jit_solution(11074965631782272705)
XLA Ops:
  6.5 0.0 all-gather.3.cloned.1.call-start
  6.5 5.5 %shard_map.82 = (bf16[384,4608]{1,0:T(8,128)(2,1)}, bf16[384,1536]{1,0:T(8,128)(2,1)}) custom-call(bf16[3,384,1536]{2,1,0:T(8,128)(2,1)} %qkv_ref.1, bf16[1536,384]{1,0:T(8,128)(2,1)} %out_ref.1), custom_call_target="tpu_custom_call" | custom-call | bytes 9437184 | tf_op jit(solution)/shard_map/pallas_call | solution.py:109
  12.1 0.0 all-gather.3.cloned.1.call-update
  12.1 0.0 all-gather.5.cloned.1.call-start
  12.1 0.7 all-gather.5.cloned.1.call-update
  12.8 3.0 collective-permute-start.1
  15.8 0.1 collective-permute-start
  15.9 0.0 copy-done.5
  15.9 0.1 slice.41
  16.0 0.1 copy.11
  16.1 0.7 reshape.30.pattern_ref
  16.8 0.1 copy.12
  16.9 0.6 reshape.33.pattern_ref
  17.5 0.0 copy-done.4
  17.5 0.3 broadcast.31.clone
  17.9 1.6 constant_dynamic-update-slice_fusion.1
  19.5 0.3 broadcast.31.clone.1
  19.8 1.6 constant_dynamic-update-slice_fusion.3
  21.5 29.9 %collective-permute-done.1 = bf16[256,3072]{1,0:T(8,128)(2,1)} collective-permute-done((bf16[256,3072]{1,0:T(8,128)(2,1)}, bf16[256,3072]{1,0:T(8,128)(2,1)}, u32[]{:S(2)}, u32[]{:S(2)}) %collective-permute-start.1) | collective-permute-done | bytes 1572896 | tf_op jit(solution)/shard_map/ppermute | solution.py:142
  51.4 32.9 %collective-permute-done = bf16[256,3072]{1,0:T(8,128)(2,1)} collective-permute-done((bf16[256,3072]{1,0:T(8,128)(2,1)}, bf16[256,3072]{1,0:T(8,128)(2,1)}, u32[]{:S(2)}, u32[]{:S(2)}) %collective-permute-start) | collective-permute-done | bytes 1572896 | tf_op jit(solution)/shard_map/ppermute | solution.py:142
  84.3 2.3 constant_dynamic-update-slice_fusion
  86.6 0.0 copy-start
  86.6 0.5 convert_reduce_fusion
  87.1 1.0 fusion.16
  88.1 5.3 %multiply_convert_fusion = (bf16[256,6144]{1,0:T(8,128)(2,1)}, f32[256,6144]{1,0:T(8,128)}) fusion(f32[6144]{0:T(1024)S(1)} %copy-done.4, f32[256]{0:T(256)S(1)} %add_rsqrt_fusion, f32[256]{0:T(256)S(1)} %broadcast_multiply_fusion, bf16[256,6144]{1,0:T(8,128)(2,1)S(1)} %get-tuple-element.35), kind=kLoop, calls=%fused_computation.19 | loop fusion | flops 7864320 | bytes 12609536 | tf_op jit(solution)/shard_map/convert_element_type | solution.py:161
  93.4 198.2 %all-gather.3.cloned.1.call-done = bf16[6144,4608]{1,0:T(8,128)(2,1)} async-done(((bf16[384,4608]{1,0:T(8,128)(2,1)}), bf16[6144,4608]{1,0:T(8,128)(2,1)}) %all-gather.3.cloned.1.call-update) | async-done | bytes 56623120 | tf_op jit(solution)/shard_map/all_gather | solution.py:139
  291.7 0.0 copy-done
  291.7 8.5 %fusion.28.up_ref = bf16[256,1152]{1,0:T(8,128)(2,1)} fusion(bf16[256,6144]{1,0:T(8,128)(2,1)S(1)} %get-tuple-element.19, bf16[6144,4608]{1,0:T(8,128)(2,1)} %all-gather.3.cloned.1.call-done), kind=kOutput, calls=%fused_computation.30 | convolution fusion | flops 3624173568 | bytes 17891328 | tf_op jit(solution)/shard_map/dot_general | solution.py:175
  300.1 0.0 copy-done.2
  300.1 20.3 %fusion.17.qkv_ref = bf16[256,3456]{1,0:T(8,128)(2,1)} fusion(bf16[256,6144]{1,0:T(8,128)(2,1)S(1)} %copy-done.2, bf16[6144,4608]{1,0:T(8,128)(2,1)} %all-gather.3.cloned.1.call-done), kind=kOutput, calls=%fused_computation.20 | convolution fusion | flops 10872520704 | bytes 47382528 | tf_op jit(solution)/shard_map/dot_general | solution.py:172
  320.4 13.4 %shard_map.83 = bf16[256,3456]{1,0:T(8,128)(2,1)} custom-call(s32[72]{0:T(128)} %reshape.30.pattern_ref, f32[1,128]{1,0:T(1,128)} %bitcast.30, f32[1,128]{1,0:T(1,128)} %bitcast.32, bf16[256,3456]{1,0:T(8,128)(2,1)} %fusion.17.qkv_ref, bf16[256,1152]{1,0:T(8,128)(2,1)} %fusion.28.up_ref), custom_call_target="tpu_custom_call" | custom-call | flops 1509949440 | bytes 4128768 | tf_op jit(solution)/shard_map/pallas_call | solution.py:73
  333.8 12.5 %fusion.4 = f32[256,3072]{1,0:T(8,128)} fusion(bf16[256,3456]{1,0:T(8,128)(2,1)} %shard_map.83, bf16[6144,4608]{1,0:T(8,128)(2,1)} %all-gather.3.cloned.1.call-done, s32[]{:T(128)S(6)} %select_n.8), kind=kOutput, calls=%fused_computation.4 | convolution fusion | flops 5435817984 | bytes 26148868 | tf_op jit(solution)/shard_map/dot_general | solution.py:182
  346.2 0.0 copy-done.7
  346.3 12.6 %fusion.2 = f32[256,3072]{1,0:T(8,128)} fusion(bf16[256,3456]{1,0:T(8,128)(2,1)S(1)} %copy-done.7, bf16[6144,4608]{1,0:T(8,128)(2,1)} %all-gather.3.cloned.1.call-done, s32[]{:T(128)S(6)} %select_n.7), kind=kOutput, calls=%fused_computation.2 | convolution fusion | flops 5435817984 | bytes 26148868 | tf_op jit(solution)/shard_map/dot_general | solution.py:182
  358.9 33.4 %all-gather.5.cloned.1.call-done = bf16[6144,1536]{1,0:T(8,128)(2,1)} async-done(((bf16[384,1536]{1,0:T(8,128)(2,1)}), bf16[6144,1536]{1,0:T(8,128)(2,1)}) %all-gather.5.cloned.1.call-update) | async-done | bytes 18874384 | tf_op jit(solution)/shard_map/all_gather | solution.py:139
  392.2 0.0 copy-done.3
  392.2 8.4 %fusion.31.qkv_ref = bf16[256,1152]{1,0:T(8,128)(2,1)} fusion(bf16[256,6144]{1,0:T(8,128)(2,1)S(1)} %copy-done.3, bf16[6144,1536]{1,0:T(8,128)(2,1)} %all-gather.5.cloned.1.call-done), kind=kOutput, calls=%fused_computation.31 | convolution fusion | flops 3624173568 | bytes 17891328 | tf_op jit(solution)/shard_map/dot_general | solution.py:172
  400.7 0.0 copy-done.1
  400.7 5.0 %fusion.34.up_ref = bf16[256,384]{1,0:T(8,128)(2,1)} fusion(bf16[256,6144]{1,0:T(8,128)(2,1)S(1)} %copy-done.1, bf16[6144,1536]{1,0:T(8,128)(2,1)} %all-gather.5.cloned.1.call-done), kind=kOutput, calls=%fused_computation.32 | convolution fusion | flops 1208057856 | bytes 8060928 | tf_op jit(solution)/shard_map/dot_general | solution.py:175
  405.7 5.5 %shard_map.84 = bf16[256,1152]{1,0:T(8,128)(2,1)} custom-call(s32[24]{0:T(128)} %reshape.33.pattern_ref, f32[1,128]{1,0:T(1,128)} %bitcast.31, f32[1,128]{1,0:T(1,128)} %bitcast.33, bf16[256,1152]{1,0:T(8,128)(2,1)} %fusion.31.qkv_ref, bf16[256,384]{1,0:T(8,128)(2,1)} %fusion.34.up_ref), custom_call_target="tpu_custom_call" | custom-call | flops 503316480 | bytes 1376256 | tf_op jit(solution)/shard_map/pallas_call | solution.py:73
  411.2 6.5 %fusion.22 = f32[256,3072]{1,0:T(8,128)S(1)} fusion(f32[256,3072]{1,0:T(8,128)} %fusion.4, bf16[256,1152]{1,0:T(8,128)(2,1)} %shard_map.84, bf16[6144,1536]{1,0:T(8,128)(2,1)} %all-gather.5.cloned.1.call-done, s32[]{:T(128)S(6)} %select_n.8), kind=kOutput, calls=%fused_computation.23 | convolution fusion | flops 1812725760 | bytes 13959172 | tf_op jit(solution)/shard_map/dot_general | solution.py:182
  417.7 0.0 slice-done
  417.7 7.0 %multiply_reduce_fusion = (f32[256]{0:T(256)S(1)}, f32[256]{0:T(256)S(1)}, f32[256]{0:T(256)S(1)}, f32[256]{0:T(256)S(1)}, bf16[256,3072]{1,0:T(8,128)(2,1)S(1)}) fusion(f32[256,6144]{1,0:T(8,128)S(1)} %bitcast.18, s32[]{:T(128)S(6)} %select_n.7, f32[3072]{0:T(1024)S(1)} %get-tuple-element.29, s32[]{:T(128)S(6)} %select_n.8, f32[256,3072]{1,0:T(8,128)S(1)} %fusion.22, ...), kind=kOutput, calls=%fused_computation.26 | convolution fusion | flops 1819802624 | bytes 21853696 | tf_op jit(solution)/shard_map/dot_general | solution.py:182
  424.7 1.4 collective-permute-start.2
  426.2 0.7 collective-permute-start.3
  426.9 34.5 %collective-permute-done.3 = f32[256,2]{0,1:T(2,128)S(1)} collective-permute-done((f32[256,2]{0,1:T(2,128)S(1)}, f32[256,2]{0,1:T(2,128)S(1)}, u32[]{:S(2)}, u32[]{:S(2)}) %collective-permute-start.3) | collective-permute-done | bytes 2080 | tf_op jit(solution)/shard_map/ppermute | solution.py:142
  461.4 0.0 collective-permute-done.2
  461.4 2.4 multiply_convert_fusion.1
  (18 shorter events, 0.1 us)
Async XLA Ops:
  6.5 285.1 %all-gather.3.cloned.1.call-start = ((), (), s32[]{:S(2)}) async-start(), calls=%async_computation | async-start | bytes 60162048 | tf_op jit(solution)/shard_map/all_gather | solution.py:139
  12.0 3.9 copy-start.5
  12.1 5.5 %copy-start.4 = (f32[6144]{0:T(1024)S(1)}, f32[6144]{0:T(1024)}, u32[]{:S(2)}) copy-start(f32[6144]{0:T(1024)} %param.10) | copy-start | bytes 73732
  12.1 380.1 %all-gather.5.cloned.1.call-start = ((), (), s32[]{:S(2)}) async-start(), calls=%async_computation.1 | async-start | bytes 20054016 | tf_op jit(solution)/shard_map/all_gather | solution.py:139
  12.8 38.5 %collective-permute-start.1 = (bf16[256,3072]{1,0:T(8,128)(2,1)}, bf16[256,3072]{1,0:T(8,128)(2,1)}, u32[]{:S(2)}, u32[]{:S(2)}) collective-permute-start(bf16[256,3072]{1,0:T(8,128)(2,1)} %param.9), channel_id=1, source_target_pairs={{0,1},{1,0},{2,3},{3,2},{4,5},{5,4},{6,7},{7,6},{8,9},{9,8},{10,11... | collective-permute-start | bytes 4718600 | tf_op jit(solution)/shard_map/ppermute | solution.py:142
  15.8 68.4 %collective-permute-start = (bf16[256,3072]{1,0:T(8,128)(2,1)}, bf16[256,3072]{1,0:T(8,128)(2,1)}, u32[]{:S(2)}, u32[]{:S(2)}) collective-permute-start(bf16[256,3072]{1,0:T(8,128)(2,1)} %param.8), channel_id=1, source_target_pairs={{0,1},{1,0},{2,3},{3,2},{4,5},{5,4},{6,7},{7,6},{8,9},{9,8},{10,11... | collective-permute-start | bytes 4718600 | tf_op jit(solution)/shard_map/ppermute | solution.py:142
  86.6 205.1 %copy-start = (bf16[256,6144]{1,0:T(8,128)(2,1)}, bf16[256,6144]{1,0:T(8,128)(2,1)S(1)}, u32[]{:S(2)}) copy-start(bf16[256,6144]{1,0:T(8,128)(2,1)S(1)} %get-tuple-element.19) | copy-start | bytes 9437188
  291.7 8.5 %copy-start.2 = (bf16[256,6144]{1,0:T(8,128)(2,1)S(1)}, bf16[256,6144]{1,0:T(8,128)(2,1)}, u32[]{:S(2)}) copy-start(bf16[256,6144]{1,0:T(8,128)(2,1)} %get-tuple-element.17) | copy-start | bytes 9437188
  333.8 12.5 %copy-start.7 = (bf16[256,3456]{1,0:T(8,128)(2,1)S(1)}, bf16[256,3456]{1,0:T(8,128)(2,1)}, u32[]{:S(2)}) copy-start(bf16[256,3456]{1,0:T(8,128)(2,1)} %shard_map.83) | copy-start | bytes 5308420
  346.2 46.0 %copy-start.3 = (bf16[256,6144]{1,0:T(8,128)(2,1)S(1)}, bf16[256,6144]{1,0:T(8,128)(2,1)}, u32[]{:S(2)}) copy-start(bf16[256,6144]{1,0:T(8,128)(2,1)} %get-tuple-element.17) | copy-start | bytes 9437188
  392.2 8.4 %copy-start.1 = (bf16[256,6144]{1,0:T(8,128)(2,1)S(1)}, bf16[256,6144]{1,0:T(8,128)(2,1)}, u32[]{:S(2)}) copy-start(bf16[256,6144]{1,0:T(8,128)(2,1)} %copy-done) | copy-start | bytes 9437188
  400.7 17.0 %slice-start = ((s8[6291456]{0:T(1024)(128)(4,1)}), s8[2097152]{0:T(1024)(128)(4,1)S(1)}, s32[]{:S(2)}) async-start(s8[6291456]{0:T(1024)(128)(4,1)} %bitcast.17), calls=%async_computation.2 | async-start | bytes 4194304
  411.2 6.5 %slice-start.1 = ((s8[6291456]{0:T(1024)(128)(4,1)}), s8[4194304]{0:T(1024)(128)(4,1)S(1)}, s32[]{:S(2)}) async-start(s8[6291456]{0:T(1024)(128)(4,1)} %bitcast.17), calls=%async_computation.3 | async-start | bytes 8388608
  411.2 6.5 %copy-start.6 = (bf16[256,1152]{1,0:T(8,128)(2,1)S(1)}, bf16[256,1152]{1,0:T(8,128)(2,1)}, u32[]{:S(2)}) copy-start(bf16[256,1152]{1,0:T(8,128)(2,1)} %shard_map.84) | copy-start | bytes 1769476
  424.7 36.7 %collective-permute-start.2 = (bf16[256,3072]{1,0:T(8,128)(2,1)S(1)}, bf16[256,3072]{1,0:T(8,128)(2,1)S(1)}, u32[]{:S(2)}, u32[]{:S(2)}) collective-permute-start(bf16[256,3072]{1,0:T(8,128)(2,1)S(1)} %get-tuple-element.27), channel_id=1, source_target_pairs={{0,1},{1,0},{2,3},{3,2},{4,5},{5,4},{6,7},{7,6},{8,9},{9,8},{10,11... | collective-permute-start | bytes 4718600 | tf_op jit(solution)/shard_map/ppermute | solution.py:142
  426.2 35.2 %collective-permute-start.3 = (f32[256,2]{0,1:T(2,128)S(1)}, f32[256,2]{0,1:T(2,128)S(1)}, u32[]{:S(2)}, u32[]{:S(2)}) collective-permute-start(f32[256,2]{0,1:T(2,128)S(1)} %maximum_add_fusion), channel_id=1, source_target_pairs={{0,1},{1,0},{2,3},{3,2},{4,5},{5,4},{6,7},{7,6},{8,9},{9,8},{10,11... | collective-permute-start | bytes 6152 | tf_op jit(solution)/shard_map/ppermute | solution.py:142
Sparse Core Ops, SparseCore 0:
  12.2 279.4 all-gather.2
  293.2 98.9 all-gather.4

commit v4 on v3

--- a/solution.py
+++ b/solution.py
@@ -123,6 +123,62 @@
     )(w_qkv, w_out)
 
 
+def projection_kernel(steps, rows_ref, grads_ref, weight_ref, qkv_ref, up_ref, qkv_sum, up_sum):
+    step = pl.program_id(0)
+    span = qkv_ref.shape[1]
+
+    @pl.when(step == 0)
+    def _():
+        qkv_sum[...] = jnp.zeros_like(qkv_sum)
+        up_sum[...] = jnp.zeros_like(up_sum)
+
+    qkv_sum[...] += jnp.dot(
+        rows_ref[...], weight_ref[:, :span], preferred_element_type=jnp.float32
+    )
+    up_sum[...] += jnp.dot(
+        grads_ref[...], weight_ref[:, span:], preferred_element_type=jnp.float32
+    )
+
+    @pl.when(step == steps - 1)
+    def _():
+        qkv_ref[...] = qkv_sum[...].astype(qkv_ref.dtype)
+        up_ref[...] = up_sum[...].astype(up_ref.dtype)
+
+
+def project(normed, grads, weight):
+    rows, depth = normed.shape
+    width = weight.shape[1] // 4
+    block = 1024 if depth % 1024 == 0 else depth
+    steps = depth // block
+    return pl.pallas_call(
+        functools.partial(projection_kernel, steps),
+        grid=(steps,),
+        out_shape=[
+            jax.ShapeDtypeStruct((rows, 3 * width), jnp.bfloat16),
+            jax.ShapeDtypeStruct((rows, width), jnp.bfloat16),
+        ],
+        in_specs=[
+            pl.BlockSpec((rows, block), lambda k: (0, k)),
+            pl.BlockSpec((rows, block), lambda k: (0, k)),
+            pl.BlockSpec((block, 4 * width), lambda k: (k, 0)),
+        ],
+        out_specs=[
+            pl.BlockSpec((rows, 3 * width), lambda k: (0, 0)),
+            pl.BlockSpec((rows, width), lambda k: (0, 0)),
+        ],
+        scratch_shapes=[
+            pltpu.VMEM((rows, 3 * width), jnp.float32),
+            pltpu.VMEM((rows, width), jnp.float32),
+        ],
+        compiler_params=pltpu.CompilerParams(vmem_limit_bytes=32 * 1024 * 1024),
+        cost_estimate=pl.CostEstimate(
+            flops=8 * rows * depth * width,
+            bytes_accessed=8 * depth * width + 4 * rows * depth,
+            transcendentals=0,
+        ),
+    )(normed, grads, weight)
+
+
 def head_chunks(heads):
     last = max(1, heads // 4)
     return [size for size in (heads - last, last) if size > 0]
@@ -166,15 +222,20 @@
 
     targets = [lax.rem(me + shift, parts) for shift in range(parts)]
     totals = [None] * parts
+    received = []
     start = 0
     for size, weight in zip(sizes, gathered):
         span = size * HD
-        qkv = jnp.dot(
-            normed, weight[:, : 3 * span], preferred_element_type=jnp.float32
-        ).astype(jnp.bfloat16)
-        upstream = jnp.dot(
-            grads_full, weight[:, 3 * span :], preferred_element_type=jnp.float32
-        ).astype(jnp.bfloat16)
+        last = start + size == local_heads
+        if last:
+            qkv, upstream = project(normed, grads_full, weight)
+        else:
+            qkv = jnp.dot(
+                normed, weight[:, : 3 * span], preferred_element_type=jnp.float32
+            ).astype(jnp.bfloat16)
+            upstream = jnp.dot(
+                grads_full, weight[:, 3 * span :], preferred_element_type=jnp.float32
+            ).astype(jnp.bfloat16)
         d_qkv = attention_grads(
             qkv, upstream, q_gain, k_gain, pattern[start : start + size]
         )
@@ -186,11 +247,15 @@
                 preferred_element_type=jnp.float32,
             )
             totals[shift] = term if totals[shift] is None else totals[shift] + term
+            if last and shift:
+                outgoing, totals[shift], d_qkv = lax.optimization_barrier(
+                    (totals[shift].astype(jnp.bfloat16), totals[shift], d_qkv)
+                )
+                received.append(exchange(outgoing, shift))
         start += size
-        if start < local_heads:
+        if not last:
             normed, grads_full, totals = lax.optimization_barrier((normed, grads_full, totals))
 
-    received = [exchange(totals[shift].astype(jnp.bfloat16), shift) for shift in range(1, parts)]
     sums = jnp.zeros((row_count, 2), jnp.float32)
     for shift in range(parts):
         gain = own_columns(input_norm_gain, targets[shift], 0)

time: 471 us -> 468 us (level)
  Pallas kernels: 24.4 us -> 35.6 us
  matrix products: 80.7 us -> 69.8 us
  waiting for transfers between devices: 330 us -> 324 us
    pallas_call x0 -> x1, Pallas kernels: none -> 11 us  [project(): pl.pallas_call(functools.partial(projection_kernel, steps), grid=(steps,)...]
    dot_general x2 -> x1, matrix products: 28.7 us -> 20.2 us  [body(): jnp.dot(normed, weight[:, :3 * span], preferred_element_type=jnp.float32)]
    dot_general x2 -> x1, matrix products: 13.5 us -> 11 us  [body(): jnp.dot(grads_full, weight[:, 3 * span:], preferred_element_type=jnp.floa...]
  transfers between devices with their start and end apart: 6 -> 6, of which waited for: 5 -> 5; matrix products, arithmetic and copies ran while one was open for 15% -> 16% of each run, Pallas kernels for 3% -> 3%
where the time goes in v4:
time: 468 us; the launch traced here: 467 us
  waiting for transfers between devices  324 us (69%)
  matrix products  69.8 us (15%)
  Pallas kernels  35.6 us (8%)
  between operations  13.6 us (3%)
  other arithmetic  9.65 us (2%)
  local copies, waits for them, and re-layouts  9.13 us (2%)
  starting transfers between devices  5.54 us (1%)
    all_gather x2, waiting for transfers between devices, body(): lax.all_gather(piece, 'dp', axis=0, tiled=True)  230 us
    ppermute x4, waiting for transfers between devices, exchange(): lax.ppermute(value, 'tensor', [(source, (source + shift) % parts) for sou...  93.6 us
    dot_general x4, matrix products, body(): lax.dot_general(d_qkv, own_columns(weight, targets[shift], 0)[:, :3 * spa...  38.6 us
    dot_general x1, matrix products, body(): jnp.dot(normed, weight[:, :3 * span], preferred_element_type=jnp.float32)  20.2 us
    pallas_call x2, Pallas kernels, attention_grads(): pl.pallas_call(functools.partial(attention_kernel, pattern.shape[2]), gri...  19.1 us
    dot_general x1, matrix products, body(): jnp.dot(grads_full, weight[:, 3 * span:], preferred_element_type=jnp.floa...  11 us
    pallas_call x1, Pallas kernels, project(): pl.pallas_call(functools.partial(projection_kernel, steps), grid=(steps,)...  11 us
  transfers between devices with their start and end apart: 6, of which 5 were waited for; matrix products, arithmetic and copies ran while one was open for 16% of the time, Pallas kernels for 3%

profile of v4, /device:TPU:0, one launch (start us, length us, event | category | flops | bytes accessed | tf_op | source)
XLA Modules:
  0.0 467.4 jit_solution(4583834632612654064)
XLA Ops:
  6.5 5.5 %shard_map.82 = (bf16[384,4608]{1,0:T(8,128)(2,1)}, bf16[384,1536]{1,0:T(8,128)(2,1)}) custom-call(bf16[3,384,1536]{2,1,0:T(8,128)(2,1)} %qkv_ref.1, bf16[1536,384]{1,0:T(8,128)(2,1)} %out_ref.1), custom_call_target="tpu_custom_call" | custom-call | bytes 9437184 | tf_op jit(solution)/shard_map/pallas_call | solution.py:109
  12.1 0.0 all-gather.3.cloned.1.call-update
  12.1 0.0 all-gather.5.cloned.1.call-start
  12.1 0.7 all-gather.5.cloned.1.call-update
  12.8 0.6 copy-done.5
  13.5 2.9 collective-permute-start.1
  16.4 0.0 copy-done.6
  16.4 0.5 collective-permute-start
  16.9 0.1 slice.35
  16.9 0.1 copy.11
  17.1 0.6 reshape.30.pattern_ref
  17.7 0.1 copy.12
  17.8 0.6 reshape.33.pattern_ref
  18.4 0.3 broadcast.31.clone
  18.8 0.2 constant_dynamic-update-slice_fusion.1
  19.0 0.3 broadcast.31.clone.1
  19.3 0.2 constant_dynamic-update-slice_fusion.3
  19.5 32.2 %collective-permute-done.1 = bf16[256,3072]{1,0:T(8,128)(2,1)} collective-permute-done((bf16[256,3072]{1,0:T(8,128)(2,1)S(1)}, bf16[256,3072]{1,0:T(8,128)(2,1)}, u32[]{:S(2)}, u32[]{:S(2)}) %collective-permute-start.1) | collective-permute-done | bytes 1572896 | tf_op jit(solution)/shard_map/ppermute | solution.py:198
  51.7 32.9 %collective-permute-done = bf16[256,3072]{1,0:T(8,128)(2,1)} collective-permute-done((bf16[256,3072]{1,0:T(8,128)(2,1)S(1)}, bf16[256,3072]{1,0:T(8,128)(2,1)}, u32[]{:S(2)}, u32[]{:S(2)}) %collective-permute-start) | collective-permute-done | bytes 1572896 | tf_op jit(solution)/shard_map/ppermute | solution.py:198
  84.6 2.3 constant_dynamic-update-slice_fusion
  86.9 0.0 copy-start
  86.9 0.0 copy-start.8
  87.0 0.5 convert_reduce_fusion
  87.5 1.0 fusion.14
  88.4 0.1 copy-done
  88.6 0.0 copy-done.8
  88.6 4.3 multiply_convert_fusion
  92.9 198.7 %all-gather.3.cloned.1.call-done = bf16[6144,4608]{1,0:T(8,128)(2,1)} async-done(((bf16[384,4608]{1,0:T(8,128)(2,1)}), bf16[6144,4608]{1,0:T(8,128)(2,1)}) %all-gather.3.cloned.1.call-update) | async-done | bytes 56623120 | tf_op jit(solution)/shard_map/all_gather | solution.py:195
  291.7 11.0 %fusion.24.up_ref = bf16[256,1152]{1,0:T(8,128)(2,1)} fusion(bf16[256,6144]{1,0:T(8,128)(2,1)} %copy-done, bf16[6144,4608]{1,0:T(8,128)(2,1)} %all-gather.3.cloned.1.call-done), kind=kOutput, calls=%fused_computation.26 | convolution fusion | flops 3624173568 | bytes 17891328 | tf_op jit(solution)/shard_map/dot_general | solution.py:236
  302.7 20.2 %fusion.15.qkv_ref = bf16[256,3456]{1,0:T(8,128)(2,1)} fusion(bf16[256,6144]{1,0:T(8,128)(2,1)S(1)} %get-tuple-element.23.rows_ref, bf16[6144,4608]{1,0:T(8,128)(2,1)} %all-gather.3.cloned.1.call-done), kind=kOutput, calls=%fused_computation.18 | convolution fusion | flops 10872520704 | bytes 47382528 | tf_op jit(solution)/shard_map/dot_general | solution.py:233
  322.9 13.4 %shard_map.83 = bf16[256,3456]{1,0:T(8,128)(2,1)} custom-call(s32[72]{0:T(128)} %reshape.30.pattern_ref, f32[1,128]{1,0:T(1,128)} %bitcast.28, f32[1,128]{1,0:T(1,128)} %bitcast.30, bf16[256,3456]{1,0:T(8,128)(2,1)} %fusion.15.qkv_ref, bf16[256,1152]{1,0:T(8,128)(2,1)} %fusion.24.up_ref), custom_call_target="tpu_custom_call" | custom-call | flops 1509949440 | bytes 4128768 | tf_op jit(solution)/shard_map/pallas_call | solution.py:73
  336.3 12.3 %fusion.2 = f32[256,3072]{1,0:T(8,128)} fusion(bf16[256,3456]{1,0:T(8,128)(2,1)} %shard_map.83, bf16[6144,4608]{1,0:T(8,128)(2,1)} %all-gather.3.cloned.1.call-done, s32[]{:T(128)S(6)} %select_n.7), kind=kOutput, calls=%fused_computation.2 | convolution fusion | flops 5435817984 | bytes 26148868 | tf_op jit(solution)/shard_map/dot_general | solution.py:243
  348.6 12.5 %fusion.4 = f32[256,3072]{1,0:T(8,128)} fusion(bf16[256,3456]{1,0:T(8,128)(2,1)S(1)} %copy-done.10, bf16[6144,4608]{1,0:T(8,128)(2,1)} %all-gather.3.cloned.1.call-done, s32[]{:T(128)S(6)} %select_n.8), kind=kOutput, calls=%fused_computation.4 | convolution fusion | flops 5435817984 | bytes 26148868 | tf_op jit(solution)/shard_map/dot_general | solution.py:243
  361.0 31.2 %all-gather.5.cloned.1.call-done.weight_ref = bf16[6144,1536]{1,0:T(8,128)(2,1)} async-done(((bf16[384,1536]{1,0:T(8,128)(2,1)}), bf16[6144,1536]{1,0:T(8,128)(2,1)}) %all-gather.5.cloned.1.call-update) | async-done | bytes 18874384 | tf_op jit(solution)/shard_map/all_gather | solution.py:195
  392.2 1.9 copy-done.1
  394.1 11.0 %shard_map.84 = (bf16[256,1152]{1,0:T(8,128)(2,1)S(1)}, bf16[256,384]{1,0:T(8,128)(2,1)S(1)}) custom-call(bf16[256,6144]{1,0:T(8,128)(2,1)S(1)} %get-tuple-element.23.rows_ref, bf16[256,6144]{1,0:T(8,128)(2,1)S(1)} %copy-done.1, bf16[6144,1536]{1,0:T(8,128)(2,1)} %all-gather.5.cloned.1.call-done.weight_ref), custom_call_target="tpu_custom_call" | custom-call | flops 4831838208 | bytes 25165824 | tf_op jit(solution)/shard_map/pallas_call | solution.py:153
  405.1 0.0 copy-start.2
  405.1 0.8 copy-done.2
  405.9 0.7 copy-done.3
  406.6 5.7 %shard_map.85 = bf16[256,1152]{1,0:T(8,128)(2,1)} custom-call(s32[24]{0:T(128)} %reshape.33.pattern_ref, f32[1,128]{1,0:T(1,128)} %bitcast.29, f32[1,128]{1,0:T(1,128)} %bitcast.31, bf16[256,1152]{1,0:T(8,128)(2,1)} %copy-done.2, bf16[256,384]{1,0:T(8,128)(2,1)} %copy-done.3), custom_call_target="tpu_custom_call" | custom-call | flops 503316480 | bytes 1376256 | tf_op jit(solution)/shard_map/pallas_call | solution.py:73
  412.3 7.6 %fusion.33 = (bf16[256,3072]{1,0:T(8,128)(2,1)}, f32[256,3072]{1,0:T(8,128)S(1)}) fusion(f32[256,3072]{1,0:T(8,128)} %fusion.2, bf16[256,1152]{1,0:T(8,128)(2,1)} %shard_map.85, bf16[6144,1536]{1,0:T(8,128)(2,1)} %all-gather.5.cloned.1.call-done.weight_ref, s32[]{:T(128)S(6)} %select_n.7), kind=kOutput, calls=%fused_computation.41 | convolution fusion | flops 1813512192 | bytes 15532036 | tf_op jit(solution)/shard_map/dot_general | solution.py:243
  419.9 1.5 collective-permute-start.2
  421.4 0.0 slice-done.1
  421.4 6.3 %multiply_reduce_fusion = (f32[256]{0:T(256)S(1)}, f32[256]{0:T(256)S(1)}, f32[256]{0:T(256)S(1)}, f32[256]{0:T(256)S(1)}, f32[256,3072]{1,0:T(8,128)S(1)}) fusion(f32[256,6144]{1,0:T(8,128)S(1)} %bitcast.16, s32[]{:T(128)S(6)} %select_n.7, f32[256,3072]{1,0:T(8,128)S(1)} %get-tuple-element.30, f32[3072]{0:T(1024)S(1)} %get-tuple-element.38, ...), kind=kOutput, calls=%fused_computation.22 | convolution fusion | flops 1819016192 | bytes 23426560 | tf_op jit(solution)/shard_map/dot_general | solution.py:243
  427.7 0.6 collective-permute-start.3
  428.3 28.5 %collective-permute-done.3 = f32[256,2]{0,1:T(2,128)S(1)} collective-permute-done((f32[256,2]{0,1:T(2,128)S(1)}, f32[256,2]{0,1:T(2,128)S(1)}, u32[]{:S(2)}, u32[]{:S(2)}) %collective-permute-start.3) | collective-permute-done | bytes 2080 | tf_op jit(solution)/shard_map/ppermute | solution.py:198
  456.8 0.0 collective-permute-done.2
  456.8 3.8 multiply_convert_fusion.1
  (23 shorter events, 0.1 us)
Async XLA Ops:
  6.5 285.1 %all-gather.3.cloned.1.call-start = ((), (), s32[]{:S(2)}) async-start(), calls=%async_computation | async-start | bytes 60162048 | tf_op jit(solution)/shard_map/all_gather | solution.py:195
  12.0 1.4 copy-start.5
  12.1 4.3 copy-start.6
  12.1 4.8 %copy-start.9 = (s32[12,4,2]{0,2,1:T(2,128)S(1)}, s32[12,4,2]{0,2,1:T(2,128)}, u32[]{:S(2)}) copy-start(s32[12,4,2]{0,2,1:T(2,128)} %param.15) | copy-start | bytes 1156
  12.1 380.1 %all-gather.5.cloned.1.call-start = ((), (), s32[]{:S(2)}) async-start(), calls=%async_computation.1 | async-start | bytes 20054016 | tf_op jit(solution)/shard_map/all_gather | solution.py:195
  13.5 38.3 %collective-permute-start.1 = (bf16[256,3072]{1,0:T(8,128)(2,1)S(1)}, bf16[256,3072]{1,0:T(8,128)(2,1)}, u32[]{:S(2)}, u32[]{:S(2)}) collective-permute-start(bf16[256,3072]{1,0:T(8,128)(2,1)S(1)} %copy-done.5), channel_id=1, source_target_pairs={{0,1},{1,0},{2,3},{3,2},{4,5},{5,4},{6,7},{7,6},{8,9},{9,8},{10,11... | collective-permute-start | bytes 4718600 | tf_op jit(solution)/shard_map/ppermute | solution.py:198
  16.4 68.2 %collective-permute-start = (bf16[256,3072]{1,0:T(8,128)(2,1)S(1)}, bf16[256,3072]{1,0:T(8,128)(2,1)}, u32[]{:S(2)}, u32[]{:S(2)}) collective-permute-start(bf16[256,3072]{1,0:T(8,128)(2,1)S(1)} %copy-done.6), channel_id=1, source_target_pairs={{0,1},{1,0},{2,3},{3,2},{4,5},{5,4},{6,7},{7,6},{8,9},{9,8},{10,11... | collective-permute-start | bytes 4718600 | tf_op jit(solution)/shard_map/ppermute | solution.py:198
  86.9 1.7 copy-start
  86.9 1.7 copy-start.8
  336.3 12.3 %copy-start.10 = (bf16[256,3456]{1,0:T(8,128)(2,1)S(1)}, bf16[256,3456]{1,0:T(8,128)(2,1)}, u32[]{:S(2)}) copy-start(bf16[256,3456]{1,0:T(8,128)(2,1)} %shard_map.83) | copy-start | bytes 5308420
  392.2 1.9 copy-start.1
  405.1 0.8 copy-start.2
  405.9 0.7 copy-start.3
  406.6 14.8 %slice-start = ((s8[6291456]{0:T(1024)(128)(4,1)}), s8[2097152]{0:T(1024)(128)(4,1)S(1)}, s32[]{:S(2)}) async-start(s8[6291456]{0:T(1024)(128)(4,1)} %bitcast.15), calls=%async_computation.2 | async-start | bytes 4194304
  412.3 9.1 %slice-start.1 = ((s8[6291456]{0:T(1024)(128)(4,1)}), s8[4194304]{0:T(1024)(128)(4,1)S(1)}, s32[]{:S(2)}) async-start(s8[6291456]{0:T(1024)(128)(4,1)} %bitcast.15), calls=%async_computation.3 | async-start | bytes 8388608
  412.3 9.1 %copy-start.4 = (f32[256,3072]{1,0:T(8,128)S(1)}, f32[256,3072]{1,0:T(8,128)}, u32[]{:S(2)}) copy-start(f32[256,3072]{1,0:T(8,128)} %fusion.4) | copy-start | bytes 9437188
  412.3 9.1 %copy-start.7 = (bf16[256,1152]{1,0:T(8,128)(2,1)S(1)}, bf16[256,1152]{1,0:T(8,128)(2,1)}, u32[]{:S(2)}) copy-start(bf16[256,1152]{1,0:T(8,128)(2,1)} %shard_map.85) | copy-start | bytes 1769476
  419.9 36.9 %collective-permute-start.2 = (bf16[256,3072]{1,0:T(8,128)(2,1)}, bf16[256,3072]{1,0:T(8,128)(2,1)}, u32[]{:S(2)}, u32[]{:S(2)}) collective-permute-start(bf16[256,3072]{1,0:T(8,128)(2,1)} %get-tuple-element.29), channel_id=1, source_target_pairs={{0,1},{1,0},{2,3},{3,2},{4,5},{5,4},{6,7},{7,6},{8,9},{9,8},{10,11... | collective-permute-start | bytes 4718600 | tf_op jit(solution)/shard_map/ppermute | solution.py:198
  427.7 29.1 %collective-permute-start.3 = (f32[256,2]{0,1:T(2,128)S(1)}, f32[256,2]{0,1:T(2,128)S(1)}, u32[]{:S(2)}, u32[]{:S(2)}) collective-permute-start(f32[256,2]{0,1:T(2,128)S(1)} %maximum_add_fusion), channel_id=1, source_target_pairs={{0,1},{1,0},{2,3},{3,2},{4,5},{5,4},{6,7},{7,6},{8,9},{9,8},{10,11... | collective-permute-start | bytes 6152 | tf_op jit(solution)/shard_map/ppermute | solution.py:198
Sparse Core Ops, SparseCore 0:
  12.2 279.4 all-gather.2
  293.3 98.9 all-gather.4
